TPU v7x, 256 devices: a whole 4x4x8 slice. The times are simulated.
256 devices in a mesh: seq: 64 (over x, z, core), ch: 4 (over y).
Axes of the slice: x: 4, y: 4, z: 8, core: 2. Of those that a mesh axis runs over, the one named last changes fastest.
Arguments:
- gate_rows: bfloat16 [32768, 2048], P(('seq', 'ch')), may hold values from -6 to 6
- key_rows: bfloat16 [32768, 2048], P(('seq', 'ch')), may hold values from -6 to 6
- value_rows: bfloat16 [32768, 2048], P(('seq', 'ch')), may hold values from -6 to 6
- spectrum: float32 [2, 128, 512, 2048], P(None, 'seq', None, 'ch'), may hold values from -6 to 6
- skip_bias: float32 [2048], replicated, may hold values from -1 to 1
Outputs:
- gated: bfloat16 [32768, 2048], P(('seq', 'ch'))
All inputs are finite; a program needn't handle non-finite values.
Results may differ from a plain program's by a relative error of at most 0.0049.
Values may be sent and summed in bfloat16 or wider, within the bound.
A program may use at most 128 MiB of HBM per device.

v0:
```python
import math

import jax
import jax.numpy as jnp
import numpy as np
from jax import lax
from jax.sharding import PartitionSpec as P

f32, bf16 = jnp.float32, jnp.bfloat16


def phase_table(first, second, modulus):
    turns = first[:, None] * second[None, :] % modulus
    angles = turns.astype(f32) * (2.0 * math.pi / modulus)
    return (jnp.cos(angles), jnp.sin(angles))


def dot(eq, a, b):
    return jnp.einsum(eq, a.astype(bf16), b.astype(bf16), preferred_element_type=f32)


def convolve(product, spectrum):
    seq_count = lax.axis_size("seq")
    tokens, width = product.shape
    length_two = 2 * seq_count * tokens
    offsets = jnp.arange(2 * seq_count, dtype=jnp.int32)
    places = jnp.arange(seq_count, dtype=jnp.int32)
    residues = jnp.arange(tokens, dtype=jnp.int32)
    off_cos, off_sin = phase_table(offsets, places, 2 * seq_count)
    res_cos, res_sin = phase_table(residues, residues, tokens)
    block = tokens // seq_count
    device = lax.axis_index("seq")
    values = lax.all_to_all(product.reshape(1, tokens, width), "seq", split_axis=1, concat_axis=0, tiled=True)
    off = jnp.stack([off_cos, -off_sin], 1)
    part = dot("kip,prc->kirc", off, values)
    own_rows = device * block + jnp.arange(block, dtype=jnp.int32)
    tw_cos, tw_sin = phase_table(offsets, own_rows, length_two)
    tw_cos = tw_cos[:, :, None]
    tw_sin = tw_sin[:, :, None]
    part = jnp.stack([part[:, 0] * tw_cos + part[:, 1] * tw_sin, part[:, 1] * tw_cos - part[:, 0] * tw_sin], 1)
    part = lax.all_to_all(part.astype(bf16), "seq", split_axis=0, concat_axis=2, tiled=True)
    table = jnp.stack([jnp.stack([res_cos, res_sin], 0), jnp.stack([-res_sin, res_cos], 0)], 0)
    nxt = dot("oisr,girc->gosc", table, part)
    re, im = nxt[:, 0], nxt[:, 1]
    spec_real, spec_imag = spectrum[0], spectrum[1]
    filt = jnp.stack([re * spec_real - im * spec_imag, re * spec_imag + im * spec_real], 1)
    back = dot("oisr,gosc->girc", table, filt)
    own_offsets = 2 * device + jnp.arange(2, dtype=jnp.int32)
    un_cos, un_sin = phase_table(own_offsets, residues, length_two)
    un_cos = un_cos[:, :, None]
    un_sin = un_sin[:, :, None]
    back = jnp.stack([back[:, 0] * un_cos - back[:, 1] * un_sin, back[:, 1] * un_cos + back[:, 0] * un_sin], 1)
    back = lax.all_to_all(back.astype(bf16), "seq", split_axis=2, concat_axis=0, tiled=True)
    field = dot("kip,kirc->prc", off, back) / length_two
    field = lax.all_to_all(field.astype(bf16), "seq", split_axis=0, concat_axis=1, tiled=True)
    return field.reshape(tokens, width)


def per_device(gate_rows, key_rows, value_rows, spectrum, skip_bias):
    product = (key_rows.astype(f32) * value_rows.astype(f32)).astype(bf16)
    cols = lax.all_to_all(product, "ch", split_axis=1, concat_axis=0, tiled=True)
    field = convolve(cols, spectrum)
    field = lax.all_to_all(field, "ch", split_axis=0, concat_axis=1, tiled=True)
    gated = gate_rows.astype(f32) * (field.astype(f32) + skip_bias[None, :] * product.astype(f32))
    return gated.astype(bf16)


def solution(mesh):
    placed = (
        P(("seq", "ch"), None),
        P(("seq", "ch"), None),
        P(("seq", "ch"), None),
        P(None, "seq", None, "ch"),
        P(),
    )
    return jax.shard_map(
        per_device, mesh=mesh, in_specs=placed, out_specs=P(("seq", "ch"), None), check_vma=False
    )
```

profile of v0, /device:TPU:1, one launch (start us, length us, event | category | flops | bytes accessed | tf_op | source)
XLA Modules:
  0.0 231.2 jit_solution(8587661304348707398)
XLA Ops:
  0.0 1.3 copy.53
  1.3 1.3 copy.54
  2.8 13.4 %all_to_all.86 = bf16[128,4,512]{0,2,1:T(8,128)(2,1)S(1)} all-to-all(bf16[128,4,512]{0,2,1:T(8,128)(2,1)S(1)} %bitcast.98), channel_id=1, replica_groups=mesh['seq'=64,'ch'=4] {'ch'}, dimensions={1} | all-to-all | bytes 1048576 | tf_op jit(solution)/shard_map/all_to_all | solution.py:61
  17.7 3.8 %reduce = bf16[512,512]{1,0:T(8,128)(2,1)S(1)} reduce(bf16[512,1,512]{2,1,0:T(2,128)(2,1)S(1)} %bitcast.100, bf16[]{:T(256)} %broadcast.368), dimensions={1}, to_apply=%bitcast.96.reduce_sub_computation | reduce | bytes 1048578
  22.5 13.3 %all-to-all-start.1 = ((bf16[64,2,2048]{2,1,0:T(2,128)(2,1)}), bf16[64,2,2048]{2,1,0:T(2,128)(2,1)S(1)}, u32[]{:S(2)}, u32[]{:S(2)}) async-start(bf16[64,2,2048]{2,1,0:T(2,128)(2,1)} %reshape.296), calls=%async_computation.1 | async-start | bytes 1048576 | tf_op jit(solution)/shard_map/all_to_all | solution.py:33
  36.2 17.0 %all-to-all-done.1 = bf16[64,2,2048]{2,1,0:T(2,128)(2,1)S(1)} async-done(((bf16[64,2,2048]{2,1,0:T(2,128)(2,1)}), bf16[64,2,2048]{2,1,0:T(2,128)(2,1)S(1)}, u32[]{:S(2)}, u32[]{:S(2)}) %all-to-all-start.1) | async-done | bytes 524320 | tf_op jit(solution)/shard_map/all_to_all | solution.py:33
  55.4 2.5 %copy.58 = bf16[128,2,8,512]{3,2,1,0:T(8,128)(2,1)} copy(bf16[128,2,8,512]{3,0,2,1:T(8,128)(2,1)S(1)} %pad_maximum_fusion) | data formatting | bytes 4194304 | tf_op jit(solution)/shard_map/stack | solution.py:40
  57.9 6.5 %all-to-all-start.2 = ((bf16[128,2,8,512]{3,2,1,0:T(8,128)(2,1)}), bf16[128,2,8,512]{3,2,1,0:T(8,128)(2,1)}, u32[]{:S(2)}, u32[]{:S(2)}) async-start(bf16[128,2,8,512]{3,2,1,0:T(8,128)(2,1)} %copy.58), calls=%async_computation.2 | async-start | bytes 4194304 | tf_op jit(solution)/shard_map/all_to_all | solution.py:41
  64.4 4.6 %fusion.50 = (f32[1,2,512,512]{3,2,1,0:T(8,128)}, f32[1,2,512,512]{3,2,1,0:T(8,128)}) fusion(f32[2,2,512,512]{3,2,1,0:T(8,128)} %param.8), kind=kLoop, calls=%fused_computation.91 | loop fusion | bytes 8388608 | tf_op jit(solution)/shard_map/slice | solution.py:45
  69.0 1.9 copy.79
  71.0 2.9 %copy.80 = f32[1,2,512,512]{2,3,1,0:T(8,128)} copy(f32[1,2,512,512]{3,2,1,0:T(8,128)} %get-tuple-element.12) | data formatting | bytes 4194304
  73.9 4.0 %fusion.25 = bf16[1,512,512]{2,1,0:T(8,128)(2,1)S(1)} fusion(), kind=kLoop, calls=%fused_computation.52 | loop fusion | flops 3932160 | bytes 524288 | tf_op jit(solution)/shard_map/convert.13
  77.8 4.3 %negate_convert_fusion = (bf16[1,512,512]{2,1,0:T(8,128)(2,1)S(1)}, bf16[1,512,512]{2,1,0:T(8,128)(2,1)S(1)}) fusion(), kind=kLoop, calls=%fused_computation.41 | loop fusion | flops 4456448 | bytes 1048576 | tf_op jit(solution)/shard_map/convert.9
  82.2 1.5 maximum_bitcast_fusion.2
  83.9 31.6 %all-to-all-done.2 = bf16[128,2,8,512]{3,2,1,0:T(8,128)(2,1)} async-done(((bf16[128,2,8,512]{3,2,1,0:T(8,128)(2,1)}), bf16[128,2,8,512]{3,2,1,0:T(8,128)(2,1)}, u32[]{:S(2)}, u32[]{:S(2)}) %all-to-all-start.2) | async-done | bytes 2097184 | tf_op jit(solution)/shard_map/all_to_all | solution.py:41
  115.5 4.7 %convolution_bitcast_fusion.1 = f32[2,2,512,512]{2,3,1,0:T(8,128)S(1)} fusion(bf16[2,2,64,8,512]{4,3,1,0,2:T(8,128)(2,1)} %bitcast.7, bf16[1,2,512,512]{3,2,1,0:T(8,128)(2,1)} %get-tuple-element.14, bf16[1,2,512,512]{3,2,1,0:T(8,128)(2,1)} %get-tuple-element.13), kind=kOutput, calls=%fused_computation.1 | convolution fusion | flops 2151677952 | bytes 8388608 | tf_op jit(solution)/shard_map/oisr,girc->gosc/dot_general | solution.py:19
  121.8 2.3 %convolution_bitcast_fusion = f32[2,2,512,512]{2,3,1,0:T(8,128)S(1)} fusion(bf16[2,1,512,512]{2,3,1,0:T(8,128)(2,1)S(1)} %get-tuple-element.6, bf16[2,1,512,512]{2,3,1,0:T(8,128)(2,1)S(1)} %get-tuple-element.5, bf16[1,2,512,512]{3,2,1,0:T(8,128)(2,1)S(1)} %copy-done.2, bf16[1,2,512,512]{3,2,1,0:T(8,128)(2,1)S(1)} %copy-done.1), kind=kOutput, calls=%fused_computation | convolution fusion | flops 2152726528 | bytes 8388608 | tf_op jit(solution)/shard_map/oisr,gosc->girc/dot_general | solution.py:19
  125.0 4.0 %copy.64 = bf16[2,2,512,512]{3,1,0,2:T(2,128)(2,1)} copy(bf16[2,2,512,512]{2,3,1,0:T(8,128)(2,1)S(1)} %pad_maximum_fusion.2) | data formatting | bytes 4194304 | tf_op jit(solution)/shard_map/stack | solution.py:52
  129.1 57.1 %all_to_all.87 = bf16[2,2,512,512]{3,1,0,2:T(2,128)(2,1)S(1)} all-to-all(bf16[2,2,512,512]{3,1,0,2:T(2,128)(2,1)} %copy.64), channel_id=1, replica_groups=mesh['seq'=64,'ch'=4] {'seq'}, dimensions={2} | all-to-all | bytes 4194304 | tf_op jit(solution)/shard_map/all_to_all | solution.py:53
  186.6 3.5 %copy.66 = bf16[64,2,2,8,512]{4,1,0,2,3:T(2,128)(2,1)} copy(bf16[64,2,2,8,512]{4,3,0,2,1:T(8,128)(2,1)S(1)} %bitcast.97) | data formatting | bytes 4194304 | tf_op jit(solution)/shard_map/all_to_all | solution.py:53
  190.1 2.7 %all_to_all.76 = bf16[128,2,8,512]{3,0,1,2:T(8,128)(2,1)S(1)} reshape(bf16[64,2,2,8,512]{4,1,0,2,3:T(2,128)(2,1)} %copy.66) | data formatting | bytes 4194304 | tf_op jit(solution)/shard_map/all_to_all | solution.py:53
  193.6 23.0 %all_to_all.88 = bf16[64,8,512]{2,1,0:T(8,128)(2,1)} all-to-all(bf16[64,8,512]{2,1,0:T(8,128)(2,1)S(1)} %copy.67), channel_id=1, replica_groups=mesh['seq'=64,'ch'=4] {'seq'}, dimensions={0} | all-to-all | bytes 1048576 | tf_op jit(solution)/shard_map/all_to_all | solution.py:55
  216.7 3.5 %all-to-all-start.5 = ((bf16[4,128,512]{2,1,0:T(8,128)(2,1)}), bf16[4,128,512]{2,1,0:T(8,128)(2,1)S(1)}, u32[]{:S(2)}, u32[]{:S(2)}) async-start(bf16[4,128,512]{2,1,0:T(8,128)(2,1)} %bitcast.30), calls=%async_computation.5 | async-start | bytes 1048576 | tf_op jit(solution)/shard_map/all_to_all | solution.py:63
  220.4 9.0 %all-to-all-done.5 = bf16[4,128,512]{2,1,0:T(8,128)(2,1)S(1)} async-done(((bf16[4,128,512]{2,1,0:T(8,128)(2,1)}), bf16[4,128,512]{2,1,0:T(8,128)(2,1)S(1)}, u32[]{:S(2)}, u32[]{:S(2)}) %all-to-all-start.5) | async-done | bytes 524320 | tf_op jit(solution)/shard_map/all_to_all | solution.py:63
  (36 shorter events, 10.9 us)
Async XLA Ops:
  22.5 30.7 %all-to-all-start.1 = ((bf16[64,2,2048]{2,1,0:T(2,128)(2,1)}), bf16[64,2,2048]{2,1,0:T(2,128)(2,1)S(1)}, u32[]{:S(2)}, u32[]{:S(2)}) async-start(bf16[64,2,2048]{2,1,0:T(2,128)(2,1)} %reshape.296), calls=%async_computation.1 | async-start | bytes 1048576 | tf_op jit(solution)/shard_map/all_to_all | solution.py:33
  57.9 57.6 %all-to-all-start.2 = ((bf16[128,2,8,512]{3,2,1,0:T(8,128)(2,1)}), bf16[128,2,8,512]{3,2,1,0:T(8,128)(2,1)}, u32[]{:S(2)}, u32[]{:S(2)}) async-start(bf16[128,2,8,512]{3,2,1,0:T(8,128)(2,1)} %copy.58), calls=%async_computation.2 | async-start | bytes 4194304 | tf_op jit(solution)/shard_map/all_to_all | solution.py:41
  115.5 4.7 %copy-start = (f32[1,2,512,512]{2,3,1,0:T(8,128)S(1)}, f32[1,2,512,512]{2,3,1,0:T(8,128)}, u32[]{:S(2)}) copy-start(f32[1,2,512,512]{2,3,1,0:T(8,128)} %copy.80) | copy-start | bytes 6291460
  120.3 1.2 copy-start.1
  120.3 1.5 copy-start.2
  193.3 26.8 %copy-start.3 = (bf16[128,2048]{1,0:T(8,128)(2,1)S(1)}, bf16[128,2048]{1,0:T(8,128)(2,1)}, u32[]{:S(2)}) copy-start(bf16[128,2048]{1,0:T(8,128)(2,1)} %param.5) | copy-start | bytes 1572868
  216.7 12.7 %all-to-all-start.5 = ((bf16[4,128,512]{2,1,0:T(8,128)(2,1)}), bf16[4,128,512]{2,1,0:T(8,128)(2,1)S(1)}, u32[]{:S(2)}, u32[]{:S(2)}) async-start(bf16[4,128,512]{2,1,0:T(8,128)(2,1)} %bitcast.30), calls=%async_computation.5 | async-start | bytes 1048576 | tf_op jit(solution)/shard_map/all_to_all | solution.py:63
  220.4 9.4 %copy-start.4 = (f32[2048]{0:T(1024)S(1)}, f32[2048]{0:T(1024)}, u32[]{:S(2)}) copy-start(f32[2048]{0:T(1024)} %param.9) | copy-start | bytes 24580
where the time goes:
time: 232 us; the launch traced here: 231 us
  blocking collectives  93.5 us (40%)
  waiting for transfers between devices  57.6 us (25%)
  local copies, waits for them, and re-layouts  30.7 us (13%)
  starting transfers between devices  23.3 us (10%)
  other arithmetic  17.6 us (8%)
  matrix products  8.25 us (4%)
    all_to_all x1, blocking collectives, convolve(): lax.all_to_all(back.astype(bf16), 'seq', split_axis=2, concat_axis=0, til...  57.1 us
    all_to_all x1, waiting for transfers between devices, convolve(): lax.all_to_all(part.astype(bf16), 'seq', split_axis=0, concat_axis=2, til...  31.6 us
    all_to_all x1, blocking collectives, convolve(): lax.all_to_all(field.astype(bf16), 'seq', split_axis=0, concat_axis=1, ti...  23 us
    all_to_all x1, waiting for transfers between devices, convolve(): lax.all_to_all(product.reshape(1, tokens, width), 'seq', split_axis=1, co...  17 us
    all_to_all x1, blocking collectives, per_device(): lax.all_to_all(product, 'ch', split_axis=1, concat_axis=0, tiled=True)  13.4 us
    all_to_all x1, starting transfers between devices, convolve(): lax.all_to_all(product.reshape(1, tokens, width), 'seq', split_axis=1, co...  13.3 us
    another operation x6, other arithmetic  11 us
    unnamed x19, local copies, waits for them, and re-layouts  10.2 us
  transfers between devices with their start and end apart: 3, of which 3 were waited for; matrix products, arithmetic and copies ran while one was open for 9% of the time, Pallas kernels for 0%

commit v1 on v0

v1 whole, which is shorter than its diff:
```python
import math

import jax
import jax.numpy as jnp
import numpy as np
from jax import lax
from jax.experimental import pallas as pl
from jax.experimental.pallas import tpu as pltpu
from jax.sharding import PartitionSpec as P

f32, bf16 = jnp.float32, jnp.bfloat16
MESH = pl.DeviceIdType.MESH
NX, NZ, NC, NY = 4, 8, 2, 4
LANES = 128
CHUNKS = 2


def split(a):
    hi = a.astype(np.float32).astype(jnp.bfloat16)
    lo = (a - hi.astype(np.float64)).astype(np.float32).astype(jnp.bfloat16)
    return np.stack([hi, lo])


def tables():
    k2 = np.arange(512)
    turn = 2 * np.pi * (np.outer(k2, k2) % 512) / 512
    cs = np.stack([np.cos(turn), np.sin(turn)]).astype(np.float32).astype(jnp.bfloat16)
    kx, kc, b = np.meshgrid(np.arange(4), np.arange(2), np.arange(2), indexing="ij")
    base = (32 * kx + 2 * kc + b).reshape(16)
    pz, px, pc = np.meshgrid(np.arange(8), np.arange(4), np.arange(2), indexing="ij")
    p = (16 * px + 2 * pz + pc).reshape(64)
    mix, mix_t, twist = [], [], []
    for z in range(8):
        k1 = base + 4 * z
        turn = 2 * np.pi * (np.outer(k1, p) % 128) / 128
        w = np.stack([np.cos(turn), -np.sin(turn)], 1).reshape(32, 64)
        mix.append(split(w))
        mix_t.append(split(w.T))
        rows = []
        for x in range(4):
            r = (128 * np.arange(4)[:, None] + 32 * x + np.arange(32)[None, :]).reshape(128)
            turn = 2 * np.pi * (np.outer(k1, r) % 65536) / 65536
            rows.append(np.concatenate([np.cos(turn), np.sin(turn)]))
        twist.append(np.stack(rows))
    twist = np.stack(twist).astype(np.float32)
    k1 = np.arange(128)
    turn = 2 * np.pi * (np.outer(k1, np.arange(512)) % 65536) / 65536
    back = np.stack([np.cos(turn), np.sin(turn)]) / 65536
    back = back.reshape(2, 64, 2, 4, 128).transpose(1, 0, 2, 3, 4).reshape(64, 16, 128).astype(np.float32)
    return cs, np.stack(mix), np.stack(mix_t), twist, back


def dot(a, b):
    return jnp.dot(a, b, preferred_element_type=f32)


def kernel(
    gate_in, key_in, value_in, spec_in, cs_in, mix_in, mixt_in, twist_in, back_in, bias_ref, out_ref,
    gate_v, key_v, value_v, spec_v, cs_v, mix_s, mixt_s, twist_s, back_s,
    prod, gath, mixb, mixbt, tw, ti, ap, aa, ff, bb, cc, part, sbuf, rbuf, fs, fb,
    loc, s1s, s1r, ags, agr, s4s, s4r, s6s, s6r, rss, rsr, s9s, s9r,
):
    d = lax.axis_index("seq")
    y = lax.axis_index("ch")
    x, z, c = d // 16, (d // 2) % NZ, d % 2

    def seq_of(xx, zz, c_):
        return 16 * xx + 2 * zz + c_

    loads = [
        pltpu.make_async_copy(key_in, key_v, loc.at[0]),
        pltpu.make_async_copy(value_in, value_v, loc.at[1]),
        pltpu.make_async_copy(mix_in.at[z], mix_s, loc.at[2]),
        pltpu.make_async_copy(mixt_in.at[z], mixt_s, loc.at[3]),
        pltpu.make_async_copy(twist_in.at[z, x], twist_s, loc.at[4]),
        pltpu.make_async_copy(back_in.at[d], back_s, loc.at[5]),
        pltpu.make_async_copy(cs_in, cs_v, loc.at[6]),
        pltpu.make_async_copy(spec_in, spec_v, loc.at[7]),
        pltpu.make_async_copy(gate_in, gate_v, loc.at[8]),
    ]
    for load in loads:
        load.start()

    def peer(i):
        return (x + i // 8) % NX, (c + i // 4 % 2) % NC, (y + i % 4) % NY

    barrier = pltpu.get_barrier_semaphore()

    def greet(i, carry):
        xx, c_, yy = peer(i)
        pl.semaphore_signal(barrier, inc=1, device_id={"seq": seq_of(xx, z, c_), "ch": yy}, device_id_type=MESH)
        return carry

    lax.fori_loop(1, 32, greet, 0)
    up, down = seq_of(x, (z + 1) % NZ, c), seq_of(x, (z + NZ - 1) % NZ, c)
    for nb in (up, down):
        pl.semaphore_signal(barrier, inc=1, device_id={"seq": nb, "ch": y}, device_id_type=MESH)

    loads[0].wait()
    loads[1].wait()

    def block_columns(blk, q):
        return pl.ds(pl.multiple_of(512 * (blk // 8) + 256 * (blk // 4 % 2) + 128 * q, 128), LANES)

    for q in range(CHUNKS):
        for blk in range(32):
            rows, cols = pl.ds(32 * (blk % 4), 32), pl.ds(512 * (blk // 8) + 256 * (blk // 4 % 2) + 128 * q, LANES)
            prod[q, blk] = (key_v[rows, cols].astype(f32) * value_v[rows, cols].astype(f32)).astype(bf16)

    pl.semaphore_wait(barrier, 33)

    for q in range(CHUNKS):
        own = 8 * y + 4 * c + x
        pltpu.make_async_copy(prod.at[q, own], gath.at[q, z, 2 * x + c, y], s1r.at[q]).start()

        def spread(i, carry, q=q):
            xx, c_, yy = peer(i)
            pltpu.make_async_remote_copy(
                src_ref=prod.at[q, 8 * yy + 4 * c_ + xx],
                dst_ref=gath.at[q, z, 2 * x + c, y],
                send_sem=s1s.at[q],
                recv_sem=s1r.at[q],
                device_id={"seq": seq_of(xx, z, c_), "ch": yy},
                device_id_type=MESH,
            ).start()
            return carry

        lax.fori_loop(1, 32, spread, 0)

    for load in loads[2:6]:
        load.wait()
    big_r = lax.broadcasted_iota(jnp.int32, (512, 1024), 0) % 16
    big_c = lax.broadcasted_iota(jnp.int32, (512, 1024), 1) % 16
    e_r = (lax.broadcasted_iota(jnp.int32, (512, 32), 0) // 16 == lax.broadcasted_iota(jnp.int32, (512, 32), 1)).astype(f32).astype(bf16)
    e_c = (lax.broadcasted_iota(jnp.int32, (64, 1024), 1) // 16 == lax.broadcasted_iota(jnp.int32, (64, 1024), 0)).astype(f32).astype(bf16)
    for i in range(2):
        wide = dot(dot(e_r, mix_s[i]).astype(bf16), e_c)
        mixb[i] = jnp.where(big_r == big_c, wide, 0.0).astype(bf16)
    big_r = lax.broadcasted_iota(jnp.int32, (1024, 512), 0) % 16
    big_c = lax.broadcasted_iota(jnp.int32, (1024, 512), 1) % 16
    e_r = (lax.broadcasted_iota(jnp.int32, (1024, 64), 0) // 16 == lax.broadcasted_iota(jnp.int32, (1024, 64), 1)).astype(f32).astype(bf16)
    e_c = (lax.broadcasted_iota(jnp.int32, (32, 512), 1) // 16 == lax.broadcasted_iota(jnp.int32, (32, 512), 0)).astype(f32).astype(bf16)
    for i in range(2):
        wide = dot(dot(e_r, mixt_s[i]).astype(bf16), e_c)
        mixbt[i] = jnp.where(big_r == big_c, wide, 0.0).astype(bf16)

    def widen(k, carry):
        tw[k] = jnp.broadcast_to(twist_s[pl.ds(k, 1), :], (128, LANES)).T
        return carry

    lax.fori_loop(0, 32, widen, 0)

    def widen_back(k, carry):
        ti[k] = jnp.broadcast_to(back_s[pl.ds(k, 1), :], (128, LANES)).T
        return carry

    lax.fori_loop(0, 16, widen_back, 0)

    def wait_bytes(ref, sem):
        pltpu.make_async_copy(ref, ref, sem).wait()

    def ag_copy(q, way, s, h):
        slot = (z - (s - 1)) % NZ if way == 0 else (z + (s - 1)) % NZ
        ref = gath.at[q, slot, pl.ds(4 * h, 4)]
        return pltpu.make_async_remote_copy(
            src_ref=ref, dst_ref=ref, send_sem=ags.at[q], recv_sem=agr.at[q, way, s - 1, h],
            device_id={"seq": up if way == 0 else down, "ch": y}, device_id_type=MESH,
        )

    def ag_wait(q, way, s, h):
        slot = (z - s) % NZ if way == 0 else (z + s) % NZ
        wait_bytes(gath.at[q, slot, pl.ds(4 * h, 4)], agr.at[q, way, s - 1, h])

    def ag_begin(q):
        for h in range(2):
            for way in range(2):
                ag_copy(q, way, 1, h).start()

    def ag_step(q, s):
        for h in range(2):
            for way in range(2):
                ag_wait(q, way, s, h)
                if s < 3 or h == way:
                    ag_copy(q, way, s + 1, h).start()

    def ag_end(q):
        ag_wait(q, 0, 4, 0)
        ag_wait(q, 1, 4, 1)

    def mix(q):
        def body(v, carry):
            halves = [gath[q, :, :, v, pl.ds(16 * u, 16), :].reshape(1024, LANES) for u in range(2)]
            data = jnp.concatenate(halves, axis=1)
            got = (dot(mixb[0], data) + dot(mixb[1], data)).reshape(16, 2, 16, 2 * LANES)
            for u in range(2):
                re, im = got[:, 0, :, LANES * u : LANES * (u + 1)], got[:, 1, :, LANES * u : LANES * (u + 1)]
                rows = pl.ds(pl.multiple_of(32 * v + 16 * u, 16), 16)
                co, si = tw[pl.ds(0, 16), rows, :], tw[pl.ds(16, 16), rows, :]
                ap[q, :, 0, v, pl.ds(16 * u, 16), :] = (re * co + im * si).astype(bf16)
                ap[q, :, 1, v, pl.ds(16 * u, 16), :] = (im * co - re * si).astype(bf16)
            return carry

        lax.fori_loop(0, 4, body, 0)

    def s4_send(q):
        def to(i):
            return (x + i // 2) % NX, (c + i % 2) % NC

        own = ap.at[q, pl.ds(2 * (2 * x + c), 2)]
        pltpu.make_async_copy(own, aa.at[q, :, :, c, :, x], s4r.at[q]).start()
        for i in range(1, 8):
            xx, c_ = to(i)
            pltpu.make_async_remote_copy(
                src_ref=ap.at[q, pl.ds(2 * (2 * xx + c_), 2)], dst_ref=aa.at[q, :, :, c, :, x],
                send_sem=s4s.at[q], recv_sem=s4r.at[q],
                device_id={"seq": seq_of(xx, z, c_), "ch": y}, device_id_type=MESH,
            ).start()

    def lanes_of(ref, *at):
        return jnp.concatenate([ref[(*at, 0)], ref[(*at, 1)]], axis=-1)

    def filter_part(q, b):
        re = jnp.concatenate([aa[q, b, 0, i].reshape(512, LANES) for i in range(2)], axis=1)
        im = jnp.concatenate([aa[q, b, 1, i].reshape(512, LANES) for i in range(2)], axis=1)
        for t in range(2):
            rows = pl.ds(256 * t, 256)
            co, si = cs_v[0, rows, :], cs_v[1, rows, :]
            y_re = dot(co, re) + dot(si, im)
            y_im = dot(co, im) - dot(si, re)
            for i in range(2):
                cols = pl.ds(256 * i + 128 * q, LANES)
                h_re, h_im = spec_v[0, b, rows, cols], spec_v[1, b, rows, cols]
                part_re, part_im = y_re[:, LANES * i : LANES * (i + 1)], y_im[:, LANES * i : LANES * (i + 1)]
                ff[0, rows, pl.ds(LANES * i, LANES)] = (part_re * h_re - part_im * h_im).astype(bf16)
                ff[1, rows, pl.ds(LANES * i, LANES)] = (part_re * h_im + part_im * h_re).astype(bf16)
        re, im = ff[0], ff[1]
        for t in range(2):
            rows = pl.ds(256 * t, 256)
            co, si = cs_v[0, rows, :], cs_v[1, rows, :]
            g_re = dot(co, re) - dot(si, im)
            g_im = dot(co, im) + dot(si, re)
            for i in range(2):
                lanes = slice(LANES * i, LANES * (i + 1))
                for v in range(2):
                    t_co, t_si = ti[4 * b + 2 * t + v], ti[8 + 4 * b + 2 * t + v]
                    p_re, p_im = g_re[128 * v : 128 * (v + 1), lanes], g_im[128 * v : 128 * (v + 1), lanes]
                    bb[q, b, 0, i, 2 * t + v] = (p_re * t_co - p_im * t_si).astype(bf16).reshape(4, 32, LANES)
                    bb[q, b, 1, i, 2 * t + v] = (p_im * t_co + p_re * t_si).astype(bf16).reshape(4, 32, LANES)

    def s6_send(q):
        here = cc.at[q, pl.ds(2 * (2 * x + c), 2)]
        pltpu.make_async_copy(bb.at[q, :, :, c, :, x], here, s6r.at[q]).start()
        for i in range(1, 8):
            xx, c_ = (x + i // 2) % NX, (c + i % 2) % NC
            pltpu.make_async_remote_copy(
                src_ref=bb.at[q, :, :, c_, :, xx], dst_ref=here,
                send_sem=s6s.at[q], recv_sem=s6r.at[q],
                device_id={"seq": seq_of(xx, z, c_), "ch": y}, device_id_type=MESH,
            ).start()

    def unmix(q):
        def body(v, carry):
            halves = [cc[q, :, :, v, pl.ds(16 * u, 16), :].reshape(512, LANES) for u in range(2)]
            data = jnp.concatenate(halves, axis=1)
            got = (dot(mixbt[0], data) + dot(mixbt[1], data)).reshape(8, 8, 16, 2 * LANES)
            for u in range(2):
                part[q, :, :, v, pl.ds(16 * u, 16), :] = got[:, :, :, LANES * u : LANES * (u + 1)]
            return carry

        lax.fori_loop(0, 4, body, 0)

    def rs_step(q, s):
        for h in range(2):
            for way in range(2):
                if s == 1 and h != way:
                    continue
                target = (z + 5 - s) % NZ if way == 0 else (z + 3 + s) % NZ
                piece = pl.ds(4 * h, 4)
                has = s > 2 or (s == 2 and h == way)
                if has:
                    wait_bytes(rbuf.at[q, way, s - 2, piece], rsr.at[q, way, s - 2, h])
                for k in range(4):
                    total = part[q, target, 4 * h + k]
                    if has:
                        total = total + rbuf[q, way, s - 2, 4 * h + k].astype(f32)
                    sbuf[q, way, s - 1, 4 * h + k] = total.astype(bf16)
                pltpu.make_async_remote_copy(
                    src_ref=sbuf.at[q, way, s - 1, piece], dst_ref=rbuf.at[q, way, s - 1, piece],
                    send_sem=rss.at[q], recv_sem=rsr.at[q, way, s - 1, h],
                    device_id={"seq": up if way == 0 else down, "ch": y}, device_id_type=MESH,
                ).start()

    def rs_end(q):
        for h in range(2):
            for way in range(2):
                wait_bytes(rbuf.at[q, way, 3, pl.ds(4 * h, 4)], rsr.at[q, way, 3, h])
            for k in range(4 * h, 4 * h + 4):
                total = part[q, z, k] + (rbuf[q, 0, 3, k].astype(f32) + rbuf[q, 1, 3, k].astype(f32))
                fs[q, pl.ds(4 * k, 4)] = total.astype(bf16)
        own = 8 * y + 4 * c + x
        pltpu.make_async_copy(fs.at[q, 4 * (2 * x + c) + y], fb.at[q, own], s9r.at[q]).start()

        def give(i, carry):
            xx, c_, yy = peer(i)
            pltpu.make_async_remote_copy(
                src_ref=fs.at[q, 4 * (2 * xx + c_) + yy], dst_ref=fb.at[q, own],
                send_sem=s9s.at[q], recv_sem=s9r.at[q],
                device_id={"seq": seq_of(xx, z, c_), "ch": yy}, device_id_type=MESH,
            ).start()
            return carry

        lax.fori_loop(1, 32, give, 0)

    def finish(q):
        wait_bytes(fb.at[q], s9r.at[q])
        for blk in range(32):
            rows, cols = pl.ds(32 * (blk % 4), 32), pl.ds(512 * (blk // 8) + 256 * (blk // 4 % 2) + 128 * q, LANES)
            field = fb[q, blk].astype(f32) + bias_ref[:, cols] * prod[q, blk].astype(f32)
            out_ref[rows, cols] = (gate_v[rows, cols].astype(f32) * field).astype(bf16)

    wait_bytes(gath.at[0, z], s1r.at[0])
    ag_begin(0)
    wait_bytes(gath.at[1, z], s1r.at[1])
    ag_step(0, 1)
    ag_step(0, 2)
    ag_step(0, 3)
    ag_begin(1)
    ag_end(0)
    mix(0)
    s4_send(0)
    ag_step(1, 1)
    ag_step(1, 2)
    loads[6].wait()
    loads[7].wait()
    wait_bytes(aa.at[0], s4r.at[0])
    filter_part(0, 0)
    ag_step(1, 3)
    filter_part(0, 1)
    s6_send(0)
    ag_end(1)
    mix(1)
    s4_send(1)
    wait_bytes(cc.at[0], s6r.at[0])
    unmix(0)
    rs_step(0, 1)
    rs_step(0, 2)
    wait_bytes(aa.at[1], s4r.at[1])
    filter_part(1, 0)
    rs_step(0, 3)
    filter_part(1, 1)
    s6_send(1)
    rs_step(0, 4)
    wait_bytes(cc.at[1], s6r.at[1])
    unmix(1)
    rs_step(1, 1)
    rs_step(1, 2)
    rs_end(0)
    rs_step(1, 3)
    rs_step(1, 4)
    loads[8].wait()
    finish(0)
    rs_end(1)
    finish(1)

    for q in range(CHUNKS):
        wait_bytes(prod.at[q, pl.ds(0, 31)], s1s.at[q])
        wait_bytes(gath.at[q, pl.ds(0, 7)], ags.at[q])
        wait_bytes(ap.at[q, pl.ds(0, 14)], s4s.at[q])
        wait_bytes(cc.at[q, pl.ds(0, 14)], s6s.at[q])
        wait_bytes(gath.at[q, pl.ds(0, 7)], rss.at[q])
        wait_bytes(fs.at[q, pl.ds(0, 31)], s9s.at[q])


def per_device(gate_rows, key_rows, value_rows, spectrum, skip_bias):
    cs, mix, mix_t, twist, back = tables()
    anywhere = pl.BlockSpec(memory_space=pl.ANY)
    vmem = pl.BlockSpec(memory_space=pltpu.VMEM)
    rows, width = gate_rows.shape
    q = CHUNKS
    dma = pltpu.SemaphoreType.DMA
    return pl.pallas_call(
        kernel,
        out_shape=jax.ShapeDtypeStruct((rows, width), bf16),
        in_specs=[anywhere] * 9 + [vmem],
        out_specs=vmem,
        scratch_shapes=[
            pltpu.VMEM((rows, width), bf16),
            pltpu.VMEM((rows, width), bf16),
            pltpu.VMEM((rows, width), bf16),
            pltpu.VMEM((2, 2, 512, 512), f32),
            pltpu.VMEM((2, 512, 512), bf16),
            pltpu.VMEM((2, 32, 64), bf16),
            pltpu.VMEM((2, 64, 32), bf16),
            pltpu.VMEM((32, 128), f32),
            pltpu.VMEM((16, 128), f32),
            pltpu.VMEM((q, 32, 32, LANES), bf16),
            pltpu.VMEM((q, NZ, 8, 4, 32, LANES), bf16),
            pltpu.VMEM((2, 512, 1024), bf16),
            pltpu.VMEM((2, 1024, 512), bf16),
            pltpu.VMEM((32, 128, LANES), f32),
            pltpu.VMEM((16, 128, LANES), f32),
            pltpu.VMEM((q, 16, 2, 4, 32, LANES), bf16),
            pltpu.VMEM((q, 2, 2, 2, 4, 4, 32, LANES), bf16),
            pltpu.VMEM((2, 512, 2 * LANES), bf16),
            pltpu.VMEM((q, 2, 2, 2, 4, 4, 32, LANES), bf16),
            pltpu.VMEM((q, 16, 2, 4, 32, LANES), bf16),
            pltpu.VMEM((q, NZ, 8, 4, 32, LANES), f32),
            pltpu.VMEM((q, 2, 4, 8, 4, 32, LANES), bf16),
            pltpu.VMEM((q, 2, 4, 8, 4, 32, LANES), bf16),
            pltpu.VMEM((q, 32, 32, LANES), bf16),
            pltpu.VMEM((q, 32, 32, LANES), bf16),
            dma((9,)),
            dma((q,)), dma((q,)),
            dma((q,)), dma((q, 2, 4, 2)),
            dma((q,)), dma((q,)),
            dma((q,)), dma((q,)),
            dma((q,)), dma((q, 2, 4, 2)),
            dma((q,)), dma((q,)),
        ],
        compiler_params=pltpu.CompilerParams(
            collective_id=0, has_side_effects=True, vmem_limit_bytes=58 * 1024 * 1024
        ),
        name="hyena",
    )(gate_rows, key_rows, value_rows, spectrum, jnp.asarray(cs), jnp.asarray(mix), jnp.asarray(mix_t), jnp.asarray(twist), jnp.asarray(back), skip_bias.reshape(1, width))


def solution(mesh):
    placed = (
        P(("seq", "ch"), None),
        P(("seq", "ch"), None),
        P(("seq", "ch"), None),
        P(None, "seq", None, "ch"),
        P(),
    )
    return jax.shard_map(
        per_device, mesh=mesh, in_specs=placed, out_specs=P(("seq", "ch"), None), check_vma=False
    )
```

time: 232 us -> 144 us (0.62)
  Pallas kernels: 0 us -> 142 us
  blocking collectives: 93.5 us -> 0 us
  waiting for transfers between devices: 57.6 us -> 0 us
  local copies, waits for them, and re-layouts: 30.7 us -> 1.88 us
  starting transfers between devices: 23.3 us -> 0 us
  other arithmetic: 17.6 us -> 0 us
  matrix products: 8.25 us -> 0 us
    pallas_call x0 -> x1, Pallas kernels: none -> 142 us  [per_device(): pl.pallas_call(kernel, out_shape=jax.ShapeDtypeStruct((rows, width), bf16...]
    all_to_all x3 -> x0, blocking collectives: 93.5 us -> none  [the longest x1 57.1 us: convolve(): lax.all_to_all(back.astype(bf16), 'seq', split_axis=2, concat_axis=0, til...]
    all_to_all x3 -> x0, waiting for transfers between devices: 57.6 us -> none  [the longest x1 31.6 us: convolve(): lax.all_to_all(part.astype(bf16), 'seq', split_axis=0, concat_axis=2, til...]
    all_to_all x3 -> x0, starting transfers between devices: 23.3 us -> none  [the longest x1 13.3 us: convolve(): lax.all_to_all(product.reshape(1, tokens, width), 'seq', split_axis=1, co...]
    another operation x9 -> x0, other arithmetic: 12.9 us -> none
    unnamed x19 -> x1, local copies, waits for them, and re-layouts: 10.2 us -> 1.88 us
    dot_general x4 -> x0, matrix products: 8.25 us -> none  [dot(): jnp.einsum(eq, a.astype(bf16), b.astype(bf16), preferred_element_type=f32)]
    all_to_all x4 -> x0, local copies, waits for them, and re-layouts: 6.86 us -> none  [the longest x3 6.65 us: convolve(): lax.all_to_all(back.astype(bf16), 'seq', split_axis=2, concat_axis=0, til...]
  transfers between devices with their start and end apart: 3 -> 0, of which waited for: 3 -> 0; matrix products, arithmetic and copies ran while one was open for 9% -> 0% of each run, Pallas kernels for 0% -> 0%
where the time goes in v1:
time: 144 us
  Pallas kernels  142 us (99%)
  local copies, waits for them, and re-layouts  1.88 us (1%)
    pallas_call x1, Pallas kernels, per_device(): pl.pallas_call(kernel, out_shape=jax.ShapeDtypeStruct((rows, width), bf16...  142 us

profile of v1, /device:TPU:1, one launch (start us, length us, event | category | flops | bytes accessed | tf_op | source)
XLA Modules:
  0.0 143.9 jit_solution(2646600139599086957)
XLA Ops:
  0.0 142.0 %hyena.1 = bf16[128,2048]{1,0:T(8,128)(2,1)} custom-call(bf16[128,2048]{1,0:T(8,128)(2,1)} %gate_in.1, bf16[128,2048]{1,0:T(8,128)(2,1)} %key_in.1, bf16[128,2048]{1,0:T(8,128)(2,1)} %value_in.1, f32[2,2,512,512]{3,2,1,0:T(8,128)} %spec_in.1, bf16[2,512,512]{2,1,0:T(8,128)(2,1)} %constant.10.clone.cs_in, bf16[8,2,32,64]{3,2,1,0:T(8,128)(2,1)} %constant.11.clone.mix_in, ...), custom_call_target="tpu_custom_call" | custom-call | tf_op jit(solution)/shard_map/hyena/pallas_call | solution.py:381
  142.0 1.9 %copy.12 = bf16[128,2048]{1,0:T(8,128)(2,1)} copy(bf16[128,2048]{1,0:T(8,128)(2,1)} %hyena.1) | data formatting | bytes 1048576

commit v2 on v1

v2 whole, which is shorter than its diff:
```python
import math

import jax
import jax.numpy as jnp
import numpy as np
from jax import lax
from jax.experimental import pallas as pl
from jax.experimental.pallas import tpu as pltpu
from jax.sharding import PartitionSpec as P

f32, bf16 = jnp.float32, jnp.bfloat16
MESH = pl.DeviceIdType.MESH
NX, NZ, NC, NY = 4, 8, 2, 4
LANES = 128
CHUNKS = 2


def split(a):
    hi = a.astype(np.float32).astype(jnp.bfloat16)
    lo = (a - hi.astype(np.float64)).astype(np.float32).astype(jnp.bfloat16)
    return np.stack([hi, lo])


def tables():
    k2 = np.arange(512)
    turn = 2 * np.pi * (np.outer(k2, k2) % 512) / 512
    cs = np.stack([np.cos(turn), np.sin(turn)]).astype(np.float32).astype(jnp.bfloat16)
    kx, kc, b = np.meshgrid(np.arange(4), np.arange(2), np.arange(2), indexing="ij")
    base = (32 * kx + 2 * kc + b).reshape(16)
    pz, px, pc = np.meshgrid(np.arange(8), np.arange(4), np.arange(2), indexing="ij")
    p = (16 * px + 2 * pz + pc).reshape(64)
    mix, mix_t, twist = [], [], []
    for z in range(8):
        k1 = base + 4 * z
        turn = 2 * np.pi * (np.outer(k1, p) % 128) / 128
        w = np.stack([np.cos(turn), -np.sin(turn)], 1).reshape(32, 64)
        mix.append(split(w))
        mix_t.append(split(w.T))
        rows = []
        for x in range(4):
            r = (128 * np.arange(4)[:, None] + 32 * x + np.arange(32)[None, :]).reshape(128)
            turn = 2 * np.pi * (np.outer(k1, r) % 65536) / 65536
            rows.append(np.concatenate([np.cos(turn), np.sin(turn)]))
        twist.append(np.stack(rows))
    twist = np.stack(twist).astype(np.float32)
    k1 = np.arange(128)
    turn = 2 * np.pi * (np.outer(k1, np.arange(512)) % 65536) / 65536
    back = np.stack([np.cos(turn), np.sin(turn)]) / 65536
    back = back.reshape(2, 64, 2, 4, 128).transpose(1, 0, 2, 3, 4).reshape(64, 16, 128).astype(np.float32)
    return cs, np.stack(mix), np.stack(mix_t), twist, back


def dot(a, b):
    return jnp.dot(a, b, preferred_element_type=f32)


def kernel(
    gate_in, key_in, value_in, spec_in, cs_in, mix_in, mixt_in, twist_in, back_in, bias_ref, out_ref,
    gate_v, key_v, value_v, spec_v, cs_v, mix_s, mixt_s, twist_s, back_s,
    prod, gath, mixb, mixbt, tw, ti, ap, aa, ff, bb, cc, part, sbuf, rbuf, fs, fb,
    loc, s1s, s1r, ags, agr, s4s, s4r, s6s, s6r, rss, rsr, s9s, s9r,
):
    d = lax.axis_index("seq")
    y = lax.axis_index("ch")
    x, z, c = d // 16, (d // 2) % NZ, d % 2

    def seq_of(xx, zz, c_):
        return 16 * xx + 2 * zz + c_

    loads = [
        pltpu.make_async_copy(key_in, key_v, loc.at[0]),
        pltpu.make_async_copy(value_in, value_v, loc.at[1]),
        pltpu.make_async_copy(mix_in.at[z], mix_s, loc.at[2]),
        pltpu.make_async_copy(mixt_in.at[z], mixt_s, loc.at[3]),
        pltpu.make_async_copy(twist_in.at[z, x], twist_s, loc.at[4]),
        pltpu.make_async_copy(back_in.at[d], back_s, loc.at[5]),
        pltpu.make_async_copy(cs_in, cs_v, loc.at[6]),
        pltpu.make_async_copy(spec_in, spec_v, loc.at[7]),
        pltpu.make_async_copy(gate_in, gate_v, loc.at[8]),
    ]
    loads[0].start()
    loads[1].start()

    def peer(i):
        return (x + i // 8) % NX, (c + i // 4 % 2) % NC, (y + i % 4) % NY

    barrier = pltpu.get_barrier_semaphore()

    def greet(i, carry):
        xx, c_, yy = peer(i)
        pl.semaphore_signal(barrier, inc=1, device_id={"seq": seq_of(xx, z, c_), "ch": yy}, device_id_type=MESH)
        return carry

    lax.fori_loop(1, 32, greet, 0)
    up, down = seq_of(x, (z + 1) % NZ, c), seq_of(x, (z + NZ - 1) % NZ, c)
    for nb in (up, down):
        pl.semaphore_signal(barrier, inc=1, device_id={"seq": nb, "ch": y}, device_id_type=MESH)

    def multiply(q):
        for blk in range(32):
            rows, cols = pl.ds(32 * (blk % 4), 32), pl.ds(512 * (blk // 8) + 256 * (blk // 4 % 2) + 128 * q, LANES)
            prod[q, blk] = (key_v[rows, cols].astype(f32) * value_v[rows, cols].astype(f32)).astype(bf16)

    def wait_bytes(ref, sem):
        pltpu.make_async_copy(ref, ref, sem).wait()

    own = 8 * y + 4 * c + x
    mine = 2 * x + c
    yh, yl = y // 2, y % 2

    def spread_all(q):
        there = gath.at[q, yh, z, mine, yl]
        pltpu.make_async_copy(prod.at[q, own], there, s1r.at[q, yh]).start()

        def spread(i, carry):
            xx, c_, yy = peer(i)
            pltpu.make_async_remote_copy(
                src_ref=prod.at[q, 8 * yy + 4 * c_ + xx],
                dst_ref=there,
                send_sem=s1s.at[q],
                recv_sem=s1r.at[q, yh],
                device_id={"seq": seq_of(xx, z, c_), "ch": yy},
                device_id_type=MESH,
            ).start()
            return carry

        lax.fori_loop(1, 32, spread, 0)

    def s1_wait(q, e):
        wait_bytes(gath.at[q, e, z], s1r.at[q, e])

    def one_hot(shape, axis):
        wide = lax.broadcasted_iota(jnp.int32, shape, axis) // 16
        return (wide == lax.broadcasted_iota(jnp.int32, shape, 1 - axis)).astype(f32).astype(bf16)

    def spread_table(small, big):
        rows, cols = small.shape[1], small.shape[2]
        diagonal = (lax.broadcasted_iota(jnp.int32, (16 * rows, 16 * cols), 0) % 16) == (
            lax.broadcasted_iota(jnp.int32, (16 * rows, 16 * cols), 1) % 16
        )
        for i in range(2):
            tall = dot(one_hot((16 * rows, rows), 0), small[i]).astype(bf16)
            wide = dot(tall, one_hot((cols, 16 * cols), 1))
            big[i] = jnp.where(diagonal, wide, 0.0).astype(bf16)

    def widen(k, carry):
        tw[k] = jnp.broadcast_to(twist_s[pl.ds(k, 1), :], (128, LANES)).T
        return carry

    def widen_back(k, carry):
        ti[k] = jnp.broadcast_to(back_s[pl.ds(k, 1), :], (128, LANES)).T
        return carry

    def ag_copy(q, e, way, s, h):
        slot = (z - (s - 1)) % NZ if way == 0 else (z + (s - 1)) % NZ
        ref = gath.at[q, e, slot, pl.ds(4 * h, 4)]
        return pltpu.make_async_remote_copy(
            src_ref=ref, dst_ref=ref, send_sem=ags.at[q, e], recv_sem=agr.at[q, e, way, s - 1, h],
            device_id={"seq": up if way == 0 else down, "ch": y}, device_id_type=MESH,
        )

    def ag_wait(q, e, way, s, h):
        slot = (z - s) % NZ if way == 0 else (z + s) % NZ
        wait_bytes(gath.at[q, e, slot, pl.ds(4 * h, 4)], agr.at[q, e, way, s - 1, h])

    def ag_begin(q, e):
        for h in range(2):
            for way in range(2):
                ag_copy(q, e, way, 1, h).start()

    def ag_step(q, e, s):
        for h in range(2):
            for way in range(2):
                ag_wait(q, e, way, s, h)
                if s < 3 or h == way:
                    ag_copy(q, e, way, s + 1, h).start()

    def ag_end(q, e):
        ag_wait(q, e, 0, 4, 0)
        ag_wait(q, e, 1, 4, 1)

    def mix(q, e):
        def body(v, carry):
            halves = [gath[q, e, :, :, v, pl.ds(16 * u, 16), :].reshape(1024, LANES) for u in range(2)]
            data = jnp.concatenate(halves, axis=1)
            got = (dot(mixb[0], data) + dot(mixb[1], data)).reshape(16, 2, 16, 2 * LANES)
            for u in range(2):
                re, im = got[:, 0, :, LANES * u : LANES * (u + 1)], got[:, 1, :, LANES * u : LANES * (u + 1)]
                rows = pl.ds(pl.multiple_of(64 * e + 32 * v + 16 * u, 16), 16)
                co, si = tw[pl.ds(0, 16), rows, :], tw[pl.ds(16, 16), rows, :]
                ap[q, e, :, 0, v, pl.ds(16 * u, 16), :] = (re * co + im * si).astype(bf16)
                ap[q, e, :, 1, v, pl.ds(16 * u, 16), :] = (im * co - re * si).astype(bf16)
            return carry

        lax.fori_loop(0, 2, body, 0)

    def s4_send(q, e):
        there = aa.at[q, :, :, c, pl.ds(2 * e, 2), x]
        pltpu.make_async_copy(ap.at[q, e, pl.ds(2 * mine, 2)], there, s4r.at[q, e]).start()
        for i in range(1, 8):
            xx, c_ = (x + i // 2) % NX, (c + i % 2) % NC
            pltpu.make_async_remote_copy(
                src_ref=ap.at[q, e, pl.ds(2 * (2 * xx + c_), 2)], dst_ref=there,
                send_sem=s4s.at[q, e], recv_sem=s4r.at[q, e],
                device_id={"seq": seq_of(xx, z, c_), "ch": y}, device_id_type=MESH,
            ).start()

    def s4_wait(q):
        for e in range(2):
            wait_bytes(cc.at[q, e], s4r.at[q, e])

    def forward(q):
        for b in range(2):
            re = jnp.concatenate([aa[q, b, 0, i].reshape(512, LANES) for i in range(2)], axis=1)
            im = jnp.concatenate([aa[q, b, 1, i].reshape(512, LANES) for i in range(2)], axis=1)
            for t in range(2):
                rows = pl.ds(256 * t, 256)
                co, si = cs_v[0, rows, :], cs_v[1, rows, :]
                y_re = dot(co, re) + dot(si, im)
                y_im = dot(co, im) - dot(si, re)
                for i in range(2):
                    cols = pl.ds(256 * i + 128 * q, LANES)
                    h_re, h_im = spec_v[0, b, rows, cols], spec_v[1, b, rows, cols]
                    p_re, p_im = y_re[:, LANES * i : LANES * (i + 1)], y_im[:, LANES * i : LANES * (i + 1)]
                    ff[b, 0, rows, pl.ds(LANES * i, LANES)] = (p_re * h_re - p_im * h_im).astype(bf16)
                    ff[b, 1, rows, pl.ds(LANES * i, LANES)] = (p_re * h_im + p_im * h_re).astype(bf16)

    def inverse(q, e):
        rows = pl.ds(256 * e, 256)
        co, si = cs_v[0, rows, :], cs_v[1, rows, :]
        for b in range(2):
            re, im = ff[b, 0], ff[b, 1]
            g_re = dot(co, re) - dot(si, im)
            g_im = dot(co, im) + dot(si, re)
            for i in range(2):
                lanes = slice(LANES * i, LANES * (i + 1))
                for v in range(2):
                    t_co, t_si = ti[4 * b + 2 * e + v], ti[8 + 4 * b + 2 * e + v]
                    p_re, p_im = g_re[128 * v : 128 * (v + 1), lanes], g_im[128 * v : 128 * (v + 1), lanes]
                    bb[q, b, 0, i, 2 * e + v] = (p_re * t_co - p_im * t_si).astype(bf16).reshape(4, 32, LANES)
                    bb[q, b, 1, i, 2 * e + v] = (p_im * t_co + p_re * t_si).astype(bf16).reshape(4, 32, LANES)

    def s6_send(q, e):
        here = cc.at[q, e, pl.ds(2 * mine, 2)]
        pltpu.make_async_copy(bb.at[q, :, :, c, pl.ds(2 * e, 2), x], here, s6r.at[q, e]).start()
        for i in range(1, 8):
            xx, c_ = (x + i // 2) % NX, (c + i % 2) % NC
            pltpu.make_async_remote_copy(
                src_ref=bb.at[q, :, :, c_, pl.ds(2 * e, 2), xx], dst_ref=here,
                send_sem=s6s.at[q, e], recv_sem=s6r.at[q, e],
                device_id={"seq": seq_of(xx, z, c_), "ch": y}, device_id_type=MESH,
            ).start()

    def s6_wait(q, e):
        wait_bytes(cc.at[q, e], s6r.at[q, e])

    def unmix(q, e):
        def body(v, carry):
            halves = [cc[q, e, :, :, v, pl.ds(16 * u, 16), :].reshape(512, LANES) for u in range(2)]
            data = jnp.concatenate(halves, axis=1)
            got = (dot(mixbt[0], data) + dot(mixbt[1], data)).reshape(8, 8, 16, 2 * LANES)
            for u in range(2):
                part[q, e, :, :, v, pl.ds(16 * u, 16), :] = got[:, :, :, LANES * u : LANES * (u + 1)]
            return carry

        lax.fori_loop(0, 2, body, 0)

    def rs_step(q, e, s):
        for h in range(2):
            for way in range(2):
                if s == 1 and h != way:
                    continue
                target = (z + 5 - s) % NZ if way == 0 else (z + 3 + s) % NZ
                piece = pl.ds(4 * h, 4)
                has = s > 2 or (s == 2 and h == way)
                total = part[q, e, target, piece]
                if has:
                    wait_bytes(rbuf.at[q, e, way, s - 2, piece], rsr.at[q, e, way, s - 2, h])
                    total = total + rbuf[q, e, way, s - 2, piece].astype(f32)
                sbuf[q, e, way, s - 1, piece] = total.astype(bf16)
                pltpu.make_async_remote_copy(
                    src_ref=sbuf.at[q, e, way, s - 1, piece], dst_ref=rbuf.at[q, e, way, s - 1, piece],
                    send_sem=rss.at[q, e], recv_sem=rsr.at[q, e, way, s - 1, h],
                    device_id={"seq": up if way == 0 else down, "ch": y}, device_id_type=MESH,
                ).start()

    def rs_end(q, e):
        for h in range(2):
            piece = pl.ds(4 * h, 4)
            for way in range(2):
                wait_bytes(rbuf.at[q, e, way, 3, piece], rsr.at[q, e, way, 3, h])
            total = part[q, e, z, piece] + (rbuf[q, e, 0, 3, piece].astype(f32) + rbuf[q, e, 1, 3, piece].astype(f32))
            fs[q, e, pl.ds(8 * h, 8)] = total.astype(bf16).reshape(8, 32, LANES)

        def send(xx, c_, yy):
            pltpu.make_async_remote_copy(
                src_ref=fs.at[q, e, 2 * (2 * xx + c_) + yy - 2 * e], dst_ref=fb.at[q, own],
                send_sem=s9s.at[q], recv_sem=s9r.at[q],
                device_id={"seq": seq_of(xx, z, c_), "ch": yy}, device_id_type=MESH,
            ).start()

        def give(i, carry):
            send((x + i // 4) % NX, (c + i // 2 % 2) % NC, 2 * e + (y + i) % 2)
            return carry

        lax.fori_loop(2, 16, give, 0)
        for i in range(2):

            @pl.when(2 * e + i == y)
            def _():
                pltpu.make_async_copy(fs.at[q, e, 2 * mine + i], fb.at[q, own], s9r.at[q]).start()

            @pl.when(2 * e + i != y)
            def _():
                send(x, c, 2 * e + i)

    def finish(q):
        wait_bytes(fb.at[q], s9r.at[q])
        for blk in range(32):
            rows, cols = pl.ds(32 * (blk % 4), 32), pl.ds(512 * (blk // 8) + 256 * (blk // 4 % 2) + 128 * q, LANES)
            field = fb[q, blk].astype(f32) + bias_ref[:, cols] * prod[q, blk].astype(f32)
            out_ref[rows, cols] = (gate_v[rows, cols].astype(f32) * field).astype(bf16)

    loads[0].wait()
    loads[1].wait()
    multiply(0)
    pl.semaphore_wait(barrier, 33)
    spread_all(0)
    multiply(1)
    spread_all(1)
    for load in loads[2:]:
        load.start()
    s1_wait(0, 0)
    ag_begin(0, 0)
    s1_wait(0, 1)
    for load in loads[2:6]:
        load.wait()
    spread_table(mix_s, mixb)
    ag_step(0, 0, 1)
    lax.fori_loop(0, 32, widen, 0)
    ag_step(0, 0, 2)
    ag_begin(0, 1)
    ag_step(0, 0, 3)
    ag_end(0, 0)
    mix(0, 0)
    s4_send(0, 0)
    ag_step(0, 1, 1)
    lax.fori_loop(0, 16, widen_back, 0)
    ag_step(0, 1, 2)
    s1_wait(1, 0)
    ag_begin(1, 0)
    ag_step(0, 1, 3)
    ag_end(0, 1)
    mix(0, 1)
    s4_send(0, 1)
    ag_step(1, 0, 1)
    spread_table(mixt_s, mixbt)
    ag_step(1, 0, 2)
    s1_wait(1, 1)
    ag_begin(1, 1)
    for load in loads[6:]:
        load.wait()
    s4_wait(0)
    forward(0)
    ag_step(1, 0, 3)
    ag_end(1, 0)
    inverse(0, 0)
    s6_send(0, 0)
    ag_step(1, 1, 1)
    mix(1, 0)
    s4_send(1, 0)
    inverse(0, 1)
    s6_send(0, 1)
    ag_step(1, 1, 2)
    ag_step(1, 1, 3)
    s6_wait(0, 0)
    unmix(0, 0)
    rs_step(0, 0, 1)
    ag_end(1, 1)
    mix(1, 1)
    s4_send(1, 1)
    rs_step(0, 0, 2)
    s6_wait(0, 1)
    unmix(0, 1)
    rs_step(0, 0, 3)
    rs_step(0, 1, 1)
    rs_step(0, 0, 4)
    rs_step(0, 1, 2)
    s4_wait(1)
    forward(1)
    rs_end(0, 0)
    inverse(1, 0)
    s6_send(1, 0)
    rs_step(0, 1, 3)
    inverse(1, 1)
    s6_send(1, 1)
    rs_step(0, 1, 4)
    s6_wait(1, 0)
    unmix(1, 0)
    rs_step(1, 0, 1)
    rs_end(0, 1)
    rs_step(1, 0, 2)
    s6_wait(1, 1)
    unmix(1, 1)
    rs_step(1, 0, 3)
    rs_step(1, 1, 1)
    rs_step(1, 0, 4)
    rs_step(1, 1, 2)
    rs_end(1, 0)
    rs_step(1, 1, 3)
    finish(0)
    rs_step(1, 1, 4)
    rs_end(1, 1)
    finish(1)

    for q in range(CHUNKS):
        wait_bytes(prod.at[q, pl.ds(0, 31)], s1s.at[q])
        wait_bytes(prod.at[q, pl.ds(0, 31)], s9s.at[q])
        for e in range(2):
            wait_bytes(gath.at[q, e, pl.ds(0, 7)], ags.at[q, e])
            wait_bytes(ap.at[q, e, pl.ds(0, 14)], s4s.at[q, e])
            wait_bytes(cc.at[q, e, pl.ds(0, 14)], s6s.at[q, e])
            wait_bytes(gath.at[q, e, pl.ds(0, 7)], rss.at[q, e])


def per_device(gate_rows, key_rows, value_rows, spectrum, skip_bias):
    cs, mix, mix_t, twist, back = tables()
    anywhere = pl.BlockSpec(memory_space=pl.ANY)
    vmem = pl.BlockSpec(memory_space=pltpu.VMEM)
    rows, width = gate_rows.shape
    q = CHUNKS
    dma = pltpu.SemaphoreType.DMA
    return pl.pallas_call(
        kernel,
        out_shape=jax.ShapeDtypeStruct((rows, width), bf16),
        in_specs=[anywhere] * 9 + [vmem],
        out_specs=vmem,
        scratch_shapes=[
            pltpu.VMEM((rows, width), bf16),
            pltpu.VMEM((rows, width), bf16),
            pltpu.VMEM((rows, width), bf16),
            pltpu.VMEM((2, 2, 512, 512), f32),
            pltpu.VMEM((2, 512, 512), bf16),
            pltpu.VMEM((2, 32, 64), bf16),
            pltpu.VMEM((2, 64, 32), bf16),
            pltpu.VMEM((32, 128), f32),
            pltpu.VMEM((16, 128), f32),
            pltpu.VMEM((q, 32, 32, LANES), bf16),
            pltpu.VMEM((q, 2, NZ, 8, 2, 32, LANES), bf16),
            pltpu.VMEM((2, 512, 1024), bf16),
            pltpu.VMEM((2, 1024, 512), bf16),
            pltpu.VMEM((32, 128, LANES), f32),
            pltpu.VMEM((16, 128, LANES), f32),
            pltpu.VMEM((q, 2, 16, 2, 2, 32, LANES), bf16),
            pltpu.VMEM((q, 2, 2, 2, 4, 4, 32, LANES), bf16),
            pltpu.VMEM((2, 2, 512, 2 * LANES), bf16),
            pltpu.VMEM((q, 2, 2, 2, 4, 4, 32, LANES), bf16),
            pltpu.VMEM((q, 2, 16, 2, 2, 32, LANES), bf16),
            pltpu.VMEM((q, 2, NZ, 8, 2, 32, LANES), f32),
            pltpu.VMEM((q, 2, 2, 4, 8, 2, 32, LANES), bf16),
            pltpu.VMEM((q, 2, 2, 4, 8, 2, 32, LANES), bf16),
            pltpu.VMEM((q, 2, 16, 32, LANES), bf16),
            pltpu.VMEM((q, 32, 32, LANES), bf16),
            dma((9,)),
            dma((q,)), dma((q, 2)),
            dma((q, 2)), dma((q, 2, 2, 4, 2)),
            dma((q, 2)), dma((q, 2)),
            dma((q, 2)), dma((q, 2)),
            dma((q, 2)), dma((q, 2, 2, 4, 2)),
            dma((q,)), dma((q,)),
        ],
        compiler_params=pltpu.CompilerParams(
            collective_id=0, has_side_effects=True, vmem_limit_bytes=58 * 1024 * 1024
        ),
        name="hyena",
    )(gate_rows, key_rows, value_rows, spectrum, jnp.asarray(cs), jnp.asarray(mix), jnp.asarray(mix_t), jnp.asarray(twist), jnp.asarray(back), skip_bias.reshape(1, width))


def solution(mesh):
    placed = (
        P(("seq", "ch"), None),
        P(("seq", "ch"), None),
        P(("seq", "ch"), None),
        P(None, "seq", None, "ch"),
        P(),
    )
    return jax.shard_map(
        per_device, mesh=mesh, in_specs=placed, out_specs=P(("seq", "ch"), None), check_vma=False
    )
```

time: 144 us -> 144 us (level)
  the two profiles are of different devices: /device:TPU:1 before, /device:TPU:25 now
where the time goes in v2:
time: 144 us
  Pallas kernels  142 us (99%)
  local copies, waits for them, and re-layouts  1.88 us (1%)
    pallas_call x1, Pallas kernels, per_device(): pl.pallas_call(kernel, out_shape=jax.ShapeDtypeStruct((rows, width), bf16...  142 us

profile of v2, /device:TPU:25, one launch (start us, length us, event | category | flops | bytes accessed | tf_op | source)
XLA Modules:
  0.0 143.6 jit_solution(1958451793172539051)
XLA Ops:
  0.0 141.7 %hyena.1 = bf16[128,2048]{1,0:T(8,128)(2,1)} custom-call(bf16[128,2048]{1,0:T(8,128)(2,1)} %gate_in.1, bf16[128,2048]{1,0:T(8,128)(2,1)} %key_in.1, bf16[128,2048]{1,0:T(8,128)(2,1)} %value_in.1, f32[2,2,512,512]{3,2,1,0:T(8,128)} %spec_in.1, bf16[2,512,512]{2,1,0:T(8,128)(2,1)} %constant.10.clone.cs_in, bf16[8,2,32,64]{3,2,1,0:T(8,128)(2,1)} %constant.11.clone.mix_in, ...), custom_call_target="tpu_custom_call" | custom-call | tf_op jit(solution)/shard_map/hyena/pallas_call | solution.py:433
  141.7 1.9 %copy.12 = bf16[128,2048]{1,0:T(8,128)(2,1)} copy(bf16[128,2048]{1,0:T(8,128)(2,1)} %hyena.1) | data formatting | bytes 1048576

commit v3 on v2

--- a/solution.py
+++ b/solution.py
@@ -163,17 +163,15 @@
         slot = (z - s) % NZ if way == 0 else (z + s) % NZ
         wait_bytes(gath.at[q, e, slot, pl.ds(4 * h, 4)], agr.at[q, e, way, s - 1, h])
 
-    def ag_begin(q, e):
-        for h in range(2):
-            for way in range(2):
-                ag_copy(q, e, way, 1, h).start()
-
-    def ag_step(q, e, s):
-        for h in range(2):
-            for way in range(2):
-                ag_wait(q, e, way, s, h)
-                if s < 3 or h == way:
-                    ag_copy(q, e, way, s + 1, h).start()
+    def ag_begin(q, e, h):
+        for way in range(2):
+            ag_copy(q, e, way, 1, h).start()
+
+    def ag_step(q, e, s, h):
+        for way in range(2):
+            ag_wait(q, e, way, s, h)
+            if s < 3 or h == way:
+                ag_copy(q, e, way, s + 1, h).start()
 
     def ag_end(q, e):
         ag_wait(q, e, 0, 4, 0)
@@ -265,24 +263,24 @@
 
         lax.fori_loop(0, 2, body, 0)
 
-    def rs_step(q, e, s):
-        for h in range(2):
-            for way in range(2):
-                if s == 1 and h != way:
-                    continue
-                target = (z + 5 - s) % NZ if way == 0 else (z + 3 + s) % NZ
-                piece = pl.ds(4 * h, 4)
-                has = s > 2 or (s == 2 and h == way)
-                total = part[q, e, target, piece]
-                if has:
-                    wait_bytes(rbuf.at[q, e, way, s - 2, piece], rsr.at[q, e, way, s - 2, h])
-                    total = total + rbuf[q, e, way, s - 2, piece].astype(f32)
-                sbuf[q, e, way, s - 1, piece] = total.astype(bf16)
-                pltpu.make_async_remote_copy(
-                    src_ref=sbuf.at[q, e, way, s - 1, piece], dst_ref=rbuf.at[q, e, way, s - 1, piece],
-                    send_sem=rss.at[q, e], recv_sem=rsr.at[q, e, way, s - 1, h],
-                    device_id={"seq": up if way == 0 else down, "ch": y}, device_id_type=MESH,
-                ).start()
+    def rs_step(q, e, s, h):
+        for way in range(2):
+            if s == 1 and h != way:
+                continue
+            target = (z + 5 - s) % NZ if way == 0 else (z + 3 + s) % NZ
+            piece = pl.ds(4 * h, 4)
+            has = s > 2 or (s == 2 and h == way)
+            total = part[q, e, target, piece]
+            if has:
+                wait_bytes(rbuf.at[q, e, way, s - 2, piece], rsr.at[q, e, way, s - 2, h])
+                total = total + rbuf[q, e, way, s - 2, piece].astype(f32)
+            sbuf[q, e, way, s - 1, piece] = total.astype(bf16)
+            pltpu.make_async_remote_copy(
+                src_ref=sbuf.at[q, e, way, s - 1, piece], dst_ref=rbuf.at[q, e, way, s - 1, piece],
+                send_sem=rss.at[q, e], recv_sem=rsr.at[q, e, way, s - 1, h],
+                device_id={"seq": up if way == 0 else down, "ch": y}, device_id_type=MESH,
+            ).start()
+
 
     def rs_end(q, e):
         for h in range(2):
@@ -326,90 +324,125 @@
     multiply(0)
     pl.semaphore_wait(barrier, 33)
     spread_all(0)
-    multiply(1)
-    spread_all(1)
     for load in loads[2:]:
         load.start()
     s1_wait(0, 0)
-    ag_begin(0, 0)
+    ag_begin(0, 0, 0)
+    ag_begin(0, 0, 1)
+    multiply(1)
+    spread_all(1)
     s1_wait(0, 1)
-    for load in loads[2:6]:
-        load.wait()
+    ag_begin(0, 1, 0)
+    ag_begin(0, 1, 1)
+    loads[4].wait()
+    lax.fori_loop(0, 32, widen, 0)
+    ag_step(0, 0, 1, 0)
+    ag_step(0, 0, 1, 1)
+    loads[2].wait()
     spread_table(mix_s, mixb)
-    ag_step(0, 0, 1)
-    lax.fori_loop(0, 32, widen, 0)
-    ag_step(0, 0, 2)
-    ag_begin(0, 1)
-    ag_step(0, 0, 3)
+    ag_step(0, 1, 1, 0)
+    loads[3].wait()
+    spread_table(mixt_s, mixbt)
+    ag_step(0, 1, 1, 1)
+    ag_step(0, 0, 2, 0)
+    loads[5].wait()
+    lax.fori_loop(0, 16, widen_back, 0)
+    ag_step(0, 0, 2, 1)
+    ag_step(0, 1, 2, 0)
+    ag_step(0, 1, 2, 1)
+    ag_step(0, 0, 3, 0)
+    ag_step(0, 0, 3, 1)
+    s1_wait(1, 0)
+    ag_begin(1, 0, 1)
+    ag_step(0, 1, 3, 0)
+    ag_step(0, 1, 3, 1)
+    ag_begin(1, 0, 0)
     ag_end(0, 0)
     mix(0, 0)
     s4_send(0, 0)
-    ag_step(0, 1, 1)
-    lax.fori_loop(0, 16, widen_back, 0)
-    ag_step(0, 1, 2)
-    s1_wait(1, 0)
-    ag_begin(1, 0)
-    ag_step(0, 1, 3)
+    ag_step(1, 0, 1, 1)
+    s1_wait(1, 1)
+    ag_begin(1, 1, 1)
     ag_end(0, 1)
     mix(0, 1)
     s4_send(0, 1)
-    ag_step(1, 0, 1)
-    spread_table(mixt_s, mixbt)
-    ag_step(1, 0, 2)
-    s1_wait(1, 1)
-    ag_begin(1, 1)
-    for load in loads[6:]:
+    ag_step(1, 0, 1, 0)
+    ag_begin(1, 1, 0)
+    ag_step(1, 0, 2, 1)
+    ag_step(1, 1, 1, 1)
+    ag_step(1, 0, 2, 0)
+    ag_step(1, 1, 1, 0)
+    ag_step(1, 0, 3, 1)
+    ag_step(1, 1, 2, 1)
+    for load in loads[6:8]:
         load.wait()
     s4_wait(0)
     forward(0)
-    ag_step(1, 0, 3)
-    ag_end(1, 0)
     inverse(0, 0)
     s6_send(0, 0)
-    ag_step(1, 1, 1)
+    inverse(0, 1)
+    s6_send(0, 1)
+    ag_step(1, 0, 3, 0)
+    ag_step(1, 1, 2, 0)
+    ag_step(1, 1, 3, 1)
+    ag_end(1, 0)
     mix(1, 0)
     s4_send(1, 0)
-    inverse(0, 1)
-    s6_send(0, 1)
-    ag_step(1, 1, 2)
-    ag_step(1, 1, 3)
+    ag_step(1, 1, 3, 0)
     s6_wait(0, 0)
     unmix(0, 0)
-    rs_step(0, 0, 1)
+    rs_step(0, 0, 1, 0)
+    rs_step(0, 0, 1, 1)
     ag_end(1, 1)
     mix(1, 1)
     s4_send(1, 1)
-    rs_step(0, 0, 2)
+    rs_step(0, 0, 2, 0)
+    rs_step(0, 0, 2, 1)
     s6_wait(0, 1)
     unmix(0, 1)
-    rs_step(0, 0, 3)
-    rs_step(0, 1, 1)
-    rs_step(0, 0, 4)
-    rs_step(0, 1, 2)
+    rs_step(0, 1, 1, 1)
+    rs_step(0, 1, 1, 0)
+    rs_step(0, 0, 3, 0)
+    rs_step(0, 0, 3, 1)
+    rs_step(0, 1, 2, 1)
+    rs_step(0, 1, 2, 0)
+    rs_step(0, 0, 4, 0)
+    rs_step(0, 0, 4, 1)
+    rs_step(0, 1, 3, 1)
     s4_wait(1)
     forward(1)
-    rs_end(0, 0)
     inverse(1, 0)
     s6_send(1, 0)
-    rs_step(0, 1, 3)
     inverse(1, 1)
     s6_send(1, 1)
-    rs_step(0, 1, 4)
+    rs_step(0, 1, 3, 0)
+    rs_end(0, 0)
+    rs_step(0, 1, 4, 1)
+    rs_step(0, 1, 4, 0)
     s6_wait(1, 0)
     unmix(1, 0)
-    rs_step(1, 0, 1)
+    rs_step(1, 0, 1, 1)
+    rs_step(1, 0, 1, 0)
     rs_end(0, 1)
-    rs_step(1, 0, 2)
+    rs_step(1, 0, 2, 1)
+    rs_step(1, 0, 2, 0)
     s6_wait(1, 1)
     unmix(1, 1)
-    rs_step(1, 0, 3)
-    rs_step(1, 1, 1)
-    rs_step(1, 0, 4)
-    rs_step(1, 1, 2)
+    rs_step(1, 1, 1, 1)
+    rs_step(1, 1, 1, 0)
+    rs_step(1, 0, 3, 1)
+    loads[8].wait()
+    finish(0)
+    rs_step(1, 0, 3, 0)
+    rs_step(1, 1, 2, 1)
+    rs_step(1, 1, 2, 0)
+    rs_step(1, 0, 4, 1)
+    rs_step(1, 0, 4, 0)
+    rs_step(1, 1, 3, 1)
+    rs_step(1, 1, 3, 0)
     rs_end(1, 0)
-    rs_step(1, 1, 3)
-    finish(0)
-    rs_step(1, 1, 4)
+    rs_step(1, 1, 4, 1)
+    rs_step(1, 1, 4, 0)
     rs_end(1, 1)
     finish(1)
 

time: 144 us -> 124 us (0.86)
  the two profiles are of different devices: /device:TPU:25 before, /device:TPU:1 now
where the time goes in v3:
time: 124 us; the launch traced here: 122 us
  Pallas kernels  120 us (97%)
  local copies, waits for them, and re-layouts  1.88 us (2%)
    pallas_call x1, Pallas kernels, per_device(): pl.pallas_call(kernel, out_shape=jax.ShapeDtypeStruct((rows, width), bf16...  120 us

profile of v3, /device:TPU:1, one launch (start us, length us, event | category | flops | bytes accessed | tf_op | source)
XLA Modules:
  0.0 121.7 jit_solution(12508350941229682017)
XLA Ops:
  0.0 119.8 %hyena.1 = bf16[128,2048]{1,0:T(8,128)(2,1)} custom-call(bf16[128,2048]{1,0:T(8,128)(2,1)} %gate_in.1, bf16[128,2048]{1,0:T(8,128)(2,1)} %key_in.1, bf16[128,2048]{1,0:T(8,128)(2,1)} %value_in.1, f32[2,2,512,512]{3,2,1,0:T(8,128)} %spec_in.1, bf16[2,512,512]{2,1,0:T(8,128)(2,1)} %constant.10.clone.cs_in, bf16[8,2,32,64]{3,2,1,0:T(8,128)(2,1)} %constant.11.clone.mix_in, ...), custom_call_target="tpu_custom_call" | custom-call | tf_op jit(solution)/shard_map/hyena/pallas_call | solution.py:466
  119.8 1.9 %copy.12 = bf16[128,2048]{1,0:T(8,128)(2,1)} copy(bf16[128,2048]{1,0:T(8,128)(2,1)} %hyena.1) | data formatting | bytes 1048576

commit v4 on v0

v4 whole, which is shorter than its diff:
```python
import math

import jax
import jax.numpy as jnp
import numpy as np
from jax import lax
from jax.experimental import pallas as pl
from jax.experimental.pallas import tpu as pltpu
from jax.sharding import PartitionSpec as P

f32, bf16 = jnp.float32, jnp.bfloat16
MESH = pl.DeviceIdType.MESH
NX, NZ, NC, NY = 4, 8, 2, 4
LANES = 128
PASSES = 1


def split(a):
    hi = a.astype(np.float32).astype(jnp.bfloat16)
    lo = (a - hi.astype(np.float64)).astype(np.float32).astype(jnp.bfloat16)
    return np.stack([hi, lo])


def tables():
    nn, jh, nl, yy, i = np.meshgrid(*(np.arange(k) for k in (2, 2, 2, 4, 16)), indexing="ij")
    r = (128 * yy + 64 * jh + 32 * nn + 16 * nl + i).reshape(512)
    turn = 2 * np.pi * (np.outer(r, r) % 512) / 512
    cs = np.stack([split(np.cos(turn))[:PASSES], split(np.sin(turn))[:PASSES]], 1)
    kx, kc, b = np.meshgrid(np.arange(4), np.arange(2), np.arange(2), indexing="ij")
    base = (32 * kx + 2 * kc + b).reshape(16)
    pz, px, pc = np.meshgrid(np.arange(8), np.arange(4), np.arange(2), indexing="ij")
    p = (16 * px + 2 * pz + pc).reshape(64)
    mix, mix_t, twist = [], [], []
    for z in range(8):
        k1 = base + 4 * z
        turn = 2 * np.pi * (np.outer(k1, p) % 128) / 128
        w = np.stack([np.cos(turn), -np.sin(turn)], 1).reshape(32, 64)
        mix.append(split(w))
        mix_t.append(split(w.T / 65536))
        both = []
        for r in (np.arange(128), 128 * (np.arange(128) % 4)):
            turn = 2 * np.pi * (np.outer(k1, r) % 65536) / 65536
            both.append(np.concatenate([np.cos(turn), np.sin(turn)]))
        twist.append(np.stack(both))
    return cs, np.stack(mix), np.stack(mix_t), np.stack(twist).astype(np.float32)


def dot(a, b):
    return jnp.dot(a, b, preferred_element_type=f32)


def swap(a, b):
    left = lax.broadcasted_iota(jnp.int32, a.shape, a.ndim - 1) < LANES // 2
    ra, rb = pltpu.roll(a, LANES // 2, a.ndim - 1), pltpu.roll(b, LANES // 2, a.ndim - 1)
    return jnp.where(left, a, rb), jnp.where(left, ra, b)


def kernel(
    gate_in, key_in, value_in, spec_in, cs_in, mix_in, mixt_in, twist_in, bias_ref, out_ref,
    gate_v, key_v, value_v, spec_v, cs_v, mix_s, mixt_s, twist_s,
    prod, gath, mixb, mixbt, tw, aa, yacc, ff, cc, part, sbuf, rbuf, hs, hh, fs, fb,
    loc, s1s, s1r, ags, agr, hss, hsr, rss, rsr, s9s, s9r,
):
    d = lax.axis_index("seq")
    y = lax.axis_index("ch")
    x, z, c = d // 16, (d // 2) % NZ, d % 2

    def seq_of(xx, zz, c_):
        return 16 * xx + 2 * zz + c_

    loads = [
        pltpu.make_async_copy(key_in, key_v, loc.at[0]),
        pltpu.make_async_copy(value_in, value_v, loc.at[1]),
        pltpu.make_async_copy(mix_in.at[z], mix_s, loc.at[2]),
        pltpu.make_async_copy(mixt_in.at[z], mixt_s, loc.at[3]),
        pltpu.make_async_copy(twist_in.at[z], twist_s, loc.at[4]),
        pltpu.make_async_copy(spec_in, spec_v, loc.at[5]),
        pltpu.make_async_copy(cs_in, cs_v, loc.at[6]),
        pltpu.make_async_copy(gate_in, gate_v, loc.at[7]),
    ]
    loads[0].start()
    loads[1].start()

    def peer(i):
        return (x + i // 8) % NX, (c + i // 4 % 2) % NC, (y + i % 4) % NY

    barrier = pltpu.get_barrier_semaphore()

    def greet(i, carry):
        xx, c_, yy = peer(i)
        pl.semaphore_signal(barrier, inc=1, device_id={"seq": seq_of(xx, z, c_), "ch": yy}, device_id_type=MESH)
        return carry

    lax.fori_loop(1, 32, greet, 0)
    up, down = seq_of(x, (z + 1) % NZ, c), seq_of(x, (z + NZ - 1) % NZ, c)
    for nb in (up, down):
        pl.semaphore_signal(barrier, inc=1, device_id={"seq": nb, "ch": y}, device_id_type=MESH)

    def wait_bytes(ref, sem):
        pltpu.make_async_copy(ref, ref, sem).wait()

    mine = 2 * x + c
    own = 8 * y + mine

    def product_of(rows, cols):
        return (key_v[rows, cols].astype(f32) * value_v[rows, cols].astype(f32)).astype(bf16).astype(f32)

    def multiply(g):
        for t in range(16):
            cols = pl.ds(128 * t, LANES)
            pair = swap(product_of(pl.ds(32 * g, 32), cols), product_of(pl.ds(64 + 32 * g, 32), cols))
            for i in range(2):
                prod[g, 2 * t + i] = pair[i].astype(bf16).reshape(2, 16, LANES)

    def spread_all(g):
        there = gath.at[pl.ds(2 * g, 2), z, mine, y]
        pltpu.make_async_copy(prod.at[g, own], there, s1r.at[g]).start()

        def spread(i, carry):
            xx, c_, yy = peer(i)
            pltpu.make_async_remote_copy(
                src_ref=prod.at[g, 8 * yy + 2 * xx + c_],
                dst_ref=there,
                send_sem=s1s.at[g],
                recv_sem=s1r.at[g],
                device_id={"seq": seq_of(xx, z, c_), "ch": yy},
                device_id_type=MESH,
            ).start()
            return carry

        lax.fori_loop(1, 32, spread, 0)

    def s1_wait(g):
        wait_bytes(gath.at[pl.ds(2 * g, 2), z], s1r.at[g])

    def one_hot(shape, axis):
        wide = lax.broadcasted_iota(jnp.int32, shape, axis) // 16
        return (wide == lax.broadcasted_iota(jnp.int32, shape, 1 - axis)).astype(f32).astype(bf16)

    def spread_table(small, big):
        rows, cols = small.shape[1], small.shape[2]
        diagonal = (lax.broadcasted_iota(jnp.int32, (16 * rows, 16 * cols), 0) % 16) == (
            lax.broadcasted_iota(jnp.int32, (16 * rows, 16 * cols), 1) % 16
        )
        for i in range(2):
            tall = dot(one_hot((16 * rows, rows), 0), small[i]).astype(bf16)
            wide = dot(tall, one_hot((cols, 16 * cols), 1))
            big[i] = jnp.where(diagonal, wide, 0.0).astype(bf16)

    def widen(k, carry):
        left = lax.broadcasted_iota(jnp.int32, (64, LANES), 1) < LANES // 2
        columns = [jnp.broadcast_to(twist_s[0, pl.ds(k + 16 * i, 1), :], (128, LANES)).T for i in range(2)]
        co, si = (jnp.where(left, a[:64], a[64:]) for a in columns)
        turns = [twist_s[1, pl.ds(k + 16 * i, 1), :] for i in range(2)]
        for v in range(4):
            t_co, t_si = (jnp.broadcast_to(a[:, v : v + 1], (64, LANES)) for a in turns)
            tw[k, v] = co * t_co - si * t_si
            tw[16 + k, v] = si * t_co + co * t_si
        return carry

    def repack(m, carry):
        row = pl.multiple_of(128 * (m % 4) + 64 * (m // 8 % 2) + 32 * (m // 16) + 16 * (m // 4 % 2), 16)
        to = pl.ds(pl.multiple_of(16 * m, 16), 16)
        for t in range(4):
            for i in range(2):
                at = pl.ds(row, 16), pl.ds(128 * t, LANES)
                pair = swap(spec_v[(i, 0, *at)], spec_v[(i, 1, *at)])
                for k in range(2):
                    hs[2 * t + k, i, to, :] = pair[k].astype(bf16)
        return carry

    def filter_send():
        pltpu.make_async_copy(hs.at[mine], hh.at[mine], hsr).start()
        for i in range(1, 8):
            xx, c_ = (x + i // 2) % NX, (c + i % 2) % NC
            pltpu.make_async_remote_copy(
                src_ref=hs.at[2 * xx + c_], dst_ref=hh.at[mine], send_sem=hss, recv_sem=hsr,
                device_id={"seq": seq_of(xx, z, c_), "ch": y}, device_id_type=MESH,
            ).start()

    def ag_copy(n, way, s, h):
        slot = (z - (s - 1)) % NZ if way == 0 else (z + (s - 1)) % NZ
        ref = gath.at[n, slot, pl.ds(4 * h, 4)]
        return pltpu.make_async_remote_copy(
            src_ref=ref, dst_ref=ref, send_sem=ags.at[n], recv_sem=agr.at[n, way, s - 1, h],
            device_id={"seq": up if way == 0 else down, "ch": y}, device_id_type=MESH,
        )

    def ag_wait(n, way, s, h):
        slot = (z - s) % NZ if way == 0 else (z + s) % NZ
        wait_bytes(gath.at[n, slot, pl.ds(4 * h, 4)], agr.at[n, way, s - 1, h])

    def ag_begin(n, h):
        for way in range(2):
            ag_copy(n, way, 1, h).start()

    def ag_step(n, s, h):
        for way in range(2):
            ag_wait(n, way, s, h)
            if s < 3 or h == way:
                ag_copy(n, way, s + 1, h).start()

    def ag_end(n):
        ag_wait(n, 0, 4, 0)
        ag_wait(n, 1, 4, 1)

    def mix(n):
        def body(v, carry):
            halves = [gath[n, :, :, 2 * v + u].reshape(1024, LANES) for u in range(2)]
            data = jnp.concatenate(halves, axis=1)
            got = (dot(mixb[0], data) + dot(mixb[1], data)).reshape(8, 2, 2, 16, 2 * LANES)
            for u in range(2):
                lanes = slice(LANES * u, LANES * (u + 1))
                pairs = []
                for b in range(2):
                    re, im = got[:, b, 0, :, lanes], got[:, b, 1, :, lanes]
                    at = 2 * v + u, pl.ds(16 * n, 16)
                    co = jnp.stack([tw[(2 * k + b, *at)] for k in range(8)])
                    si = jnp.stack([tw[(16 + 2 * k + b, *at)] for k in range(8)])
                    pairs.append((re * co + im * si, im * co - re * si))
                for i in range(2):
                    for jh, tile in enumerate(swap(pairs[0][i], pairs[1][i])):
                        aa[i, :, n // 2, jh, n % 2, 2 * v + u] = tile.astype(bf16)
            return carry

        lax.fori_loop(0, 2, body, 0)

    def forward(g, w):
        re, im = (
            jnp.concatenate([aa[i, 2 * w + k, g].reshape(256, LANES) for k in range(2)], axis=1) for i in range(2)
        )
        y_re, y_im = (yacc[i, w] if g else 0.0 for i in range(2))
        for k in range(PASSES):
            co, si = cs_v[k, 0, :, pl.ds(256 * g, 256)], cs_v[k, 1, :, pl.ds(256 * g, 256)]
            y_re = y_re + (dot(co, re) + dot(si, im))
            y_im = y_im + (dot(co, im) - dot(si, re))
        if g == 0:
            yacc[0, w] = y_re
            yacc[1, w] = y_im
            return
        h_re, h_im = (
            jnp.concatenate([hh[2 * w + k, i] for k in range(2)], axis=1).astype(f32) for i in range(2)
        )
        ff[0, w] = (y_re * h_re - y_im * h_im).astype(bf16)
        ff[1, w] = (y_re * h_im + y_im * h_re).astype(bf16)

    def inverse(n):
        base = 256 * (n // 2) + 64 * (n % 2)
        tabs = [
            [jnp.concatenate([cs_v[k, i, pl.ds(base + 128 * jh, 64), :] for jh in range(2)], axis=0) for i in range(2)]
            for k in range(PASSES)
        ]
        for w in range(4):
            re, im = ff[0, w], ff[1, w]
            g_re = g_im = 0.0
            for co, si in tabs:
                g_re = g_re + (dot(co, re) - dot(si, im))
                g_im = g_im + (dot(co, im) + dot(si, re))
            for k in range(2):
                lanes = slice(LANES * k, LANES * (k + 1))
                b_re = swap(g_re[:64, lanes], g_re[64:, lanes])
                b_im = swap(g_im[:64, lanes], g_im[64:, lanes])
                for b in range(2):
                    f = 4 * w + 2 * k + b
                    co = tw[f, :, pl.ds(16 * n, 16), :].reshape(64, LANES)
                    si = tw[16 + f, :, pl.ds(16 * n, 16), :].reshape(64, LANES)
                    cc[n, 2 * f] = (b_re[b] * co - b_im[b] * si).astype(bf16).reshape(4, 16, LANES)
                    cc[n, 2 * f + 1] = (b_im[b] * co + b_re[b] * si).astype(bf16).reshape(4, 16, LANES)

    def unmix(n):
        def body(v, carry):
            halves = [cc[n, :, 2 * v + u].reshape(512, LANES) for u in range(2)]
            data = jnp.concatenate(halves, axis=1)
            got = (dot(mixbt[0], data) + dot(mixbt[1], data)).reshape(8, 8, 16, 2 * LANES)
            for u in range(2):
                part[n, :, :, 2 * v + u] = got[:, :, :, LANES * u : LANES * (u + 1)]
            return carry

        lax.fori_loop(0, 2, body, 0)

    def rs_step(n, s, h):
        for way in range(2):
            if s == 1 and h != way:
                continue
            target = (z + 5 - s) % NZ if way == 0 else (z + 3 + s) % NZ
            piece = pl.ds(4 * h, 4)
            has = s > 2 or (s == 2 and h == way)
            total = part[n, target, piece]
            if has:
                wait_bytes(rbuf.at[n, way, s - 2, piece], rsr.at[n, way, s - 2, h])
                total = total + rbuf[n, way, s - 2, piece].astype(f32)
            sbuf[n, way, s - 1, piece] = total.astype(bf16)
            pltpu.make_async_remote_copy(
                src_ref=sbuf.at[n, way, s - 1, piece], dst_ref=rbuf.at[n, way, s - 1, piece],
                send_sem=rss.at[n], recv_sem=rsr.at[n, way, s - 1, h],
                device_id={"seq": up if way == 0 else down, "ch": y}, device_id_type=MESH,
            ).start()

    def rs_end(n):
        for h in range(2):
            piece = pl.ds(4 * h, 4)
            for way in range(2):
                wait_bytes(rbuf.at[n, way, 3, piece], rsr.at[n, way, 3, h])
            total = part[n, z, piece] + (rbuf[n, 0, 3, piece].astype(f32) + rbuf[n, 1, 3, piece].astype(f32))
            fs[n // 2, pl.ds(16 * h, 16), n % 2] = total.astype(bf16).reshape(16, 16, LANES)

    def give_all(g):
        pltpu.make_async_copy(fs.at[g, 4 * mine + y], fb.at[g, own], s9r.at[g]).start()

        def give(i, carry):
            xx, c_, yy = peer(i)
            pltpu.make_async_remote_copy(
                src_ref=fs.at[g, 4 * (2 * xx + c_) + yy], dst_ref=fb.at[g, own],
                send_sem=s9s.at[g], recv_sem=s9r.at[g],
                device_id={"seq": seq_of(xx, z, c_), "ch": yy}, device_id_type=MESH,
            ).start()
            return carry

        lax.fori_loop(1, 32, give, 0)

    def finish(g):
        wait_bytes(fb.at[g], s9r.at[g])
        for t in range(16):
            cols = pl.ds(128 * t, LANES)
            pair = swap(*(fb[g, 2 * t + i].reshape(32, LANES).astype(f32) for i in range(2)))
            for jh in range(2):
                rows = pl.ds(64 * jh + 32 * g, 32)
                field = pair[jh] + bias_ref[:, cols] * product_of(rows, cols)
                out_ref[rows, cols] = (gate_v[rows, cols].astype(f32) * field).astype(bf16)

    loads[0].wait()
    loads[1].wait()
    multiply(0)
    pl.semaphore_wait(barrier, 33)
    spread_all(0)
    for load in loads[2:]:
        load.start()
    s1_wait(0)
    ag_begin(1, 1)
    ag_begin(1, 0)
    ag_begin(0, 0)
    multiply(1)
    spread_all(1)
    ag_step(1, 1, 1)
    ag_begin(0, 1)
    loads[5].wait()
    lax.fori_loop(0, 8, repack, 0)
    ag_step(1, 1, 0)
    lax.fori_loop(16, 24, repack, 0)
    lax.fori_loop(8, 16, repack, 0)
    ag_step(0, 1, 0)
    lax.fori_loop(24, 32, repack, 0)
    filter_send()
    ag_step(1, 2, 1)
    loads[2].wait()
    spread_table(mix_s, mixb)
    ag_step(0, 1, 1)
    loads[4].wait()
    lax.fori_loop(0, 4, widen, 0)
    loads[3].wait()
    spread_table(mixt_s, mixbt)
    ag_step(1, 2, 0)
    ag_step(0, 2, 0)
    lax.fori_loop(4, 8, widen, 0)
    lax.fori_loop(12, 16, widen, 0)
    ag_step(1, 3, 1)
    lax.fori_loop(8, 12, widen, 0)
    s1_wait(1)
    ag_begin(3, 1)
    ag_step(0, 2, 1)
    ag_step(1, 3, 0)
    ag_step(0, 3, 0)
    ag_begin(3, 0)
    ag_step(3, 1, 1)
    ag_step(0, 3, 1)
    ag_end(1)
    mix(1)
    ag_begin(2, 1)
    ag_begin(2, 0)
    ag_step(3, 1, 0)
    ag_step(3, 2, 1)
    ag_end(0)
    mix(0)
    ag_step(2, 1, 1)
    loads[6].wait()
    forward(0, 1)
    forward(0, 0)
    ag_step(2, 1, 0)
    forward(0, 2)
    forward(0, 3)
    ag_step(3, 2, 0)
    ag_step(3, 3, 1)
    ag_step(2, 2, 1)
    ag_step(2, 2, 0)
    ag_step(3, 3, 0)
    ag_step(2, 3, 1)
    ag_step(2, 3, 0)
    ag_end(3)
    mix(3)
    ag_end(2)
    mix(2)
    wait_bytes(hh, hsr)
    forward(1, 0)
    forward(1, 2)
    forward(1, 1)
    forward(1, 3)
    inverse(0)
    unmix(0)
    rs_step(0, 1, 1)
    rs_step(0, 1, 0)
    inverse(1)
    inverse(2)
    rs_step(0, 2, 1)
    rs_step(0, 2, 0)
    unmix(2)
    rs_step(2, 1, 1)
    rs_step(2, 1, 0)
    rs_step(0, 3, 1)
    unmix(1)
    rs_step(0, 3, 0)
    rs_step(2, 2, 1)
    inverse(3)
    rs_step(2, 2, 0)
    unmix(3)
    rs_step(0, 4, 1)
    rs_step(0, 4, 0)
    rs_step(2, 3, 1)
    rs_step(2, 3, 0)
    rs_step(1, 1, 0)
    rs_step(1, 1, 1)
    rs_end(0)
    rs_step(3, 1, 1)
    rs_step(3, 1, 0)
    rs_step(2, 4, 1)
    rs_step(2, 4, 0)
    rs_step(1, 2, 0)
    rs_step(1, 2, 1)
    rs_step(3, 2, 1)
    rs_step(3, 2, 0)
    rs_end(2)
    rs_step(1, 3, 0)
    rs_step(1, 3, 1)
    rs_step(3, 3, 1)
    rs_step(3, 3, 0)
    rs_step(1, 4, 0)
    rs_step(1, 4, 1)
    rs_step(3, 4, 1)
    rs_step(3, 4, 0)
    rs_end(1)
    give_all(0)
    rs_end(3)
    give_all(1)
    loads[7].wait()
    finish(0)
    finish(1)

    for g in range(2):
        wait_bytes(prod.at[g, pl.ds(0, 31)], s1s.at[g])
        wait_bytes(prod.at[g, pl.ds(0, 31)], s9s.at[g])
    wait_bytes(hs.at[pl.ds(0, 7)], hss)
    for n in range(4):
        wait_bytes(gath.at[n, pl.ds(0, 7)], ags.at[n])
        wait_bytes(gath.at[n, pl.ds(0, 7)], rss.at[n])


def per_device(gate_rows, key_rows, value_rows, spectrum, skip_bias):
    cs, mix, mix_t, twist = tables()
    anywhere = pl.BlockSpec(memory_space=pl.ANY)
    vmem = pl.BlockSpec(memory_space=pltpu.VMEM)
    rows, width = gate_rows.shape
    dma = pltpu.SemaphoreType.DMA
    return pl.pallas_call(
        kernel,
        out_shape=jax.ShapeDtypeStruct((rows, width), bf16),
        in_specs=[anywhere] * 8 + [vmem],
        out_specs=vmem,
        scratch_shapes=[
            pltpu.VMEM((rows, width), bf16),
            pltpu.VMEM((rows, width), bf16),
            pltpu.VMEM((rows, width), bf16),
            pltpu.VMEM((2, 2, 512, 512), f32),
            pltpu.VMEM((PASSES, 2, 512, 512), bf16),
            pltpu.VMEM((2, 32, 64), bf16),
            pltpu.VMEM((2, 64, 32), bf16),
            pltpu.VMEM((2, 32, 128), f32),
            pltpu.VMEM((2, 32, 2, 16, LANES), bf16),
            pltpu.VMEM((4, NZ, 8, 4, 16, LANES), bf16),
            pltpu.VMEM((2, 512, 1024), bf16),
            pltpu.VMEM((2, 1024, 512), bf16),
            pltpu.VMEM((32, 4, 64, LANES), f32),
            pltpu.VMEM((2, 8, 2, 2, 2, 4, 16, LANES), bf16),
            pltpu.VMEM((2, 4, 512, 2 * LANES), f32),
            pltpu.VMEM((2, 4, 512, 2 * LANES), bf16),
            pltpu.VMEM((4, 32, 4, 16, LANES), bf16),
            pltpu.VMEM((4, NZ, 8, 4, 16, LANES), f32),
            pltpu.VMEM((4, 2, 4, 8, 4, 16, LANES), bf16),
            pltpu.VMEM((4, 2, 4, 8, 4, 16, LANES), bf16),
            pltpu.VMEM((8, 2, 512, LANES), bf16),
            pltpu.VMEM((8, 2, 512, LANES), bf16),
            pltpu.VMEM((2, 32, 2, 16, LANES), bf16),
            pltpu.VMEM((2, 32, 2, 16, LANES), bf16),
            dma((8,)),
            dma((2,)), dma((2,)),
            dma((4,)), dma((4, 2, 4, 2)),
            dma, dma,
            dma((4,)), dma((4, 2, 4, 2)),
            dma((2,)), dma((2,)),
        ],
        compiler_params=pltpu.CompilerParams(
            collective_id=0, has_side_effects=True, vmem_limit_bytes=60 * 1024 * 1024
        ),
        name="hyena",
    )(gate_rows, key_rows, value_rows, spectrum, *(jnp.asarray(t) for t in (cs, mix, mix_t, twist)), skip_bias.reshape(1, width))


def solution(mesh):
    placed = (
        P(("seq", "ch"), None),
        P(("seq", "ch"), None),
        P(("seq", "ch"), None),
        P(None, "seq", None, "ch"),
        P(),
    )
    return jax.shard_map(
        per_device, mesh=mesh, in_specs=placed, out_specs=P(("seq", "ch"), None), check_vma=False
    )
```

time: 232 us -> 119 us (0.51)
  Pallas kernels: 0 us -> 117 us
  blocking collectives: 93.5 us -> 0 us
  waiting for transfers between devices: 57.6 us -> 0 us
  local copies, waits for them, and re-layouts: 30.7 us -> 1.88 us
  starting transfers between devices: 23.3 us -> 0 us
  other arithmetic: 17.6 us -> 0 us
  matrix products: 8.25 us -> 0 us
    pallas_call x0 -> x1, Pallas kernels: none -> 117 us  [per_device(): pl.pallas_call(kernel, out_shape=jax.ShapeDtypeStruct((rows, width), bf16...]
    all_to_all x3 -> x0, blocking collectives: 93.5 us -> none  [the longest x1 57.1 us: convolve(): lax.all_to_all(back.astype(bf16), 'seq', split_axis=2, concat_axis=0, til...]
    all_to_all x3 -> x0, waiting for transfers between devices: 57.6 us -> none  [the longest x1 31.6 us: convolve(): lax.all_to_all(part.astype(bf16), 'seq', split_axis=0, concat_axis=2, til...]
    all_to_all x3 -> x0, starting transfers between devices: 23.3 us -> none  [the longest x1 13.3 us: convolve(): lax.all_to_all(product.reshape(1, tokens, width), 'seq', split_axis=1, co...]
    another operation x9 -> x0, other arithmetic: 12.9 us -> none
    unnamed x19 -> x1, local copies, waits for them, and re-layouts: 10.2 us -> 1.88 us
    dot_general x4 -> x0, matrix products: 8.25 us -> none  [dot(): jnp.einsum(eq, a.astype(bf16), b.astype(bf16), preferred_element_type=f32)]
    all_to_all x4 -> x0, local copies, waits for them, and re-layouts: 6.86 us -> none  [the longest x3 6.65 us: convolve(): lax.all_to_all(back.astype(bf16), 'seq', split_axis=2, concat_axis=0, til...]
  transfers between devices with their start and end apart: 3 -> 0, of which waited for: 3 -> 0; matrix products, arithmetic and copies ran while one was open for 9% -> 0% of each run, Pallas kernels for 0% -> 0%
where the time goes in v4:
time: 119 us
  Pallas kernels  117 us (98%)
  local copies, waits for them, and re-layouts  1.88 us (2%)
    pallas_call x1, Pallas kernels, per_device(): pl.pallas_call(kernel, out_shape=jax.ShapeDtypeStruct((rows, width), bf16...  117 us

profile of v4, /device:TPU:1, one launch (start us, length us, event | category | flops | bytes accessed | tf_op | source)
XLA Modules:
  0.0 119.3 jit_solution(5708597949909992821)
XLA Ops:
  0.0 117.4 %hyena.1 = bf16[128,2048]{1,0:T(8,128)(2,1)} custom-call(bf16[128,2048]{1,0:T(8,128)(2,1)} %gate_in.1, bf16[128,2048]{1,0:T(8,128)(2,1)} %key_in.1, bf16[128,2048]{1,0:T(8,128)(2,1)} %value_in.1, f32[2,2,512,512]{3,2,1,0:T(8,128)} %spec_in.1, bf16[1,2,512,512]{3,2,1,0:T(8,128)(2,1)} %constant.8.clone.cs_in, bf16[8,2,32,64]{3,2,1,0:T(8,128)(2,1)} %constant.9.clone.mix_in, ...), custom_call_target="tpu_custom_call" | custom-call | tf_op jit(solution)/shard_map/hyena/pallas_call | solution.py:472
  117.4 1.9 %copy.11 = bf16[128,2048]{1,0:T(8,128)(2,1)} copy(bf16[128,2048]{1,0:T(8,128)(2,1)} %hyena.1) | data formatting | bytes 1048576

commit v5 on v4

--- a/solution.py
+++ b/solution.py
@@ -22,8 +22,7 @@
 
 
 def tables():
-    nn, jh, nl, yy, i = np.meshgrid(*(np.arange(k) for k in (2, 2, 2, 4, 16)), indexing="ij")
-    r = (128 * yy + 64 * jh + 32 * nn + 16 * nl + i).reshape(512)
+    r = np.arange(512)
     turn = 2 * np.pi * (np.outer(r, r) % 512) / 512
     cs = np.stack([split(np.cos(turn))[:PASSES], split(np.sin(turn))[:PASSES]], 1)
     kx, kc, b = np.meshgrid(np.arange(4), np.arange(2), np.arange(2), indexing="ij")
@@ -81,17 +80,28 @@
     loads[0].start()
     loads[1].start()
 
-    def peer(i):
-        return (x + i // 8) % NX, (c + i // 4 % 2) % NC, (y + i % 4) % NY
+    xs = [lax.rem(x + i, NX) for i in range(NX)]
+    cores = [c, 1 - c]
+    plane = [(2 * xx + c_, seq_of(xx, z, c_)) for xx in xs for c_ in cores]
+
+    def each_peer(act):
+        for place, seq in plane[1:]:
+            act(place, seq, y)
+
+        def others(i, carry):
+            yy = lax.rem(y + i, NY)
+            for place, seq in plane:
+                act(place, seq, yy)
+            return carry
+
+        lax.fori_loop(1, NY, others, 0)
 
     barrier = pltpu.get_barrier_semaphore()
 
-    def greet(i, carry):
-        xx, c_, yy = peer(i)
-        pl.semaphore_signal(barrier, inc=1, device_id={"seq": seq_of(xx, z, c_), "ch": yy}, device_id_type=MESH)
-        return carry
-
-    lax.fori_loop(1, 32, greet, 0)
+    def greet(place, seq, yy):
+        pl.semaphore_signal(barrier, inc=1, device_id={"seq": seq, "ch": yy}, device_id_type=MESH)
+
+    each_peer(greet)
     up, down = seq_of(x, (z + 1) % NZ, c), seq_of(x, (z + NZ - 1) % NZ, c)
     for nb in (up, down):
         pl.semaphore_signal(barrier, inc=1, device_id={"seq": nb, "ch": y}, device_id_type=MESH)
@@ -102,36 +112,38 @@
     mine = 2 * x + c
     own = 8 * y + mine
 
+    after = [lax.rem(y + k, NY) for k in range(NY)]
+    before = [lax.rem(y + NY - k, NY) for k in range(NY)]
+
+    def columns_of(yy, t):
+        return pl.ds(pl.multiple_of(512 * yy + 128 * t, 128), LANES)
+
     def product_of(rows, cols):
         return (key_v[rows, cols].astype(f32) * value_v[rows, cols].astype(f32)).astype(bf16).astype(f32)
 
-    def multiply(g):
-        for t in range(16):
-            cols = pl.ds(128 * t, LANES)
-            pair = swap(product_of(pl.ds(32 * g, 32), cols), product_of(pl.ds(64 + 32 * g, 32), cols))
+    def multiply(k):
+        for t in range(4):
+            cols = columns_of(before[k], t)
+            pair = swap(product_of(pl.ds(0, 64), cols), product_of(pl.ds(64, 64), cols))
             for i in range(2):
-                prod[g, 2 * t + i] = pair[i].astype(bf16).reshape(2, 16, LANES)
-
-    def spread_all(g):
-        there = gath.at[pl.ds(2 * g, 2), z, mine, y]
-        pltpu.make_async_copy(prod.at[g, own], there, s1r.at[g]).start()
-
-        def spread(i, carry):
-            xx, c_, yy = peer(i)
+                prod[8 * before[k] + 2 * t + i] = pair[i].astype(bf16)
+
+    def spread_all(k):
+        there = gath.at[k, z, mine]
+        if k == 0:
+            pltpu.make_async_copy(prod.at[own], there, s1r.at[k]).start()
+        for place, seq in plane[k == 0 :]:
             pltpu.make_async_remote_copy(
-                src_ref=prod.at[g, 8 * yy + 2 * xx + c_],
+                src_ref=prod.at[8 * before[k] + place],
                 dst_ref=there,
-                send_sem=s1s.at[g],
-                recv_sem=s1r.at[g],
-                device_id={"seq": seq_of(xx, z, c_), "ch": yy},
+                send_sem=s1s,
+                recv_sem=s1r.at[k],
+                device_id={"seq": seq, "ch": before[k]},
                 device_id_type=MESH,
             ).start()
-            return carry
-
-        lax.fori_loop(1, 32, spread, 0)
-
-    def s1_wait(g):
-        wait_bytes(gath.at[pl.ds(2 * g, 2), z], s1r.at[g])
+
+    def s1_wait(k):
+        wait_bytes(gath.at[k, z], s1r.at[k])
 
     def one_hot(shape, axis):
         wide = lax.broadcasted_iota(jnp.int32, shape, axis) // 16
@@ -159,23 +171,21 @@
         return carry
 
     def repack(m, carry):
-        row = pl.multiple_of(128 * (m % 4) + 64 * (m // 8 % 2) + 32 * (m // 16) + 16 * (m // 4 % 2), 16)
-        to = pl.ds(pl.multiple_of(16 * m, 16), 16)
+        rows = pl.ds(pl.multiple_of(16 * m, 16), 16)
         for t in range(4):
             for i in range(2):
-                at = pl.ds(row, 16), pl.ds(128 * t, LANES)
+                at = rows, pl.ds(128 * t, LANES)
                 pair = swap(spec_v[(i, 0, *at)], spec_v[(i, 1, *at)])
                 for k in range(2):
-                    hs[2 * t + k, i, to, :] = pair[k].astype(bf16)
+                    hs[2 * t + k, i, rows, :] = pair[k].astype(bf16)
         return carry
 
     def filter_send():
         pltpu.make_async_copy(hs.at[mine], hh.at[mine], hsr).start()
-        for i in range(1, 8):
-            xx, c_ = (x + i // 2) % NX, (c + i % 2) % NC
+        for place, seq in plane[1:]:
             pltpu.make_async_remote_copy(
-                src_ref=hs.at[2 * xx + c_], dst_ref=hh.at[mine], send_sem=hss, recv_sem=hsr,
-                device_id={"seq": seq_of(xx, z, c_), "ch": y}, device_id_type=MESH,
+                src_ref=hs.at[place], dst_ref=hh.at[mine], send_sem=hss, recv_sem=hsr,
+                device_id={"seq": seq, "ch": y}, device_id_type=MESH,
             ).start()
 
     def ag_copy(n, way, s, h):
@@ -206,7 +216,8 @@
 
     def mix(n):
         def body(v, carry):
-            halves = [gath[n, :, :, 2 * v + u].reshape(1024, LANES) for u in range(2)]
+            rows = [pl.ds(pl.multiple_of(32 * v + 16 * u, 16), 16) for u in range(2)]
+            halves = [gath[n, :, :, rows[u], :].reshape(1024, LANES) for u in range(2)]
             data = jnp.concatenate(halves, axis=1)
             got = (dot(mixb[0], data) + dot(mixb[1], data)).reshape(8, 2, 2, 16, 2 * LANES)
             for u in range(2):
@@ -214,24 +225,31 @@
                 pairs = []
                 for b in range(2):
                     re, im = got[:, b, 0, :, lanes], got[:, b, 1, :, lanes]
-                    at = 2 * v + u, pl.ds(16 * n, 16)
+                    at = after[n], rows[u]
                     co = jnp.stack([tw[(2 * k + b, *at)] for k in range(8)])
                     si = jnp.stack([tw[(16 + 2 * k + b, *at)] for k in range(8)])
                     pairs.append((re * co + im * si, im * co - re * si))
                 for i in range(2):
                     for jh, tile in enumerate(swap(pairs[0][i], pairs[1][i])):
-                        aa[i, :, n // 2, jh, n % 2, 2 * v + u] = tile.astype(bf16)
+                        aa[i, :, after[n], jh, rows[u], :] = tile.astype(bf16)
             return carry
 
         lax.fori_loop(0, 2, body, 0)
 
     def forward(g, w):
+        both = after[2 * g : 2 * g + 2]
         re, im = (
-            jnp.concatenate([aa[i, 2 * w + k, g].reshape(256, LANES) for k in range(2)], axis=1) for i in range(2)
+            jnp.concatenate(
+                [jnp.concatenate([aa[i, 2 * w + k, yy].reshape(128, LANES) for k in range(2)], axis=1) for yy in both], axis=0
+            )
+            for i in range(2)
         )
         y_re, y_im = (yacc[i, w] if g else 0.0 for i in range(2))
         for k in range(PASSES):
-            co, si = cs_v[k, 0, :, pl.ds(256 * g, 256)], cs_v[k, 1, :, pl.ds(256 * g, 256)]
+            co, si = (
+                jnp.concatenate([cs_v[k, i, :, pl.ds(pl.multiple_of(128 * yy, 128), 128)] for yy in both], axis=1)
+                for i in range(2)
+            )
             y_re = y_re + (dot(co, re) + dot(si, im))
             y_im = y_im + (dot(co, im) - dot(si, re))
         if g == 0:
@@ -245,11 +263,8 @@
         ff[1, w] = (y_re * h_im + y_im * h_re).astype(bf16)
 
     def inverse(n):
-        base = 256 * (n // 2) + 64 * (n % 2)
-        tabs = [
-            [jnp.concatenate([cs_v[k, i, pl.ds(base + 128 * jh, 64), :] for jh in range(2)], axis=0) for i in range(2)]
-            for k in range(PASSES)
-        ]
+        rows = pl.ds(pl.multiple_of(128 * after[n], 128), 128)
+        tabs = [[cs_v[k, i, rows, :] for i in range(2)] for k in range(PASSES)]
         for w in range(4):
             re, im = ff[0, w], ff[1, w]
             g_re = g_im = 0.0
@@ -262,18 +277,19 @@
                 b_im = swap(g_im[:64, lanes], g_im[64:, lanes])
                 for b in range(2):
                     f = 4 * w + 2 * k + b
-                    co = tw[f, :, pl.ds(16 * n, 16), :].reshape(64, LANES)
-                    si = tw[16 + f, :, pl.ds(16 * n, 16), :].reshape(64, LANES)
-                    cc[n, 2 * f] = (b_re[b] * co - b_im[b] * si).astype(bf16).reshape(4, 16, LANES)
-                    cc[n, 2 * f + 1] = (b_im[b] * co + b_re[b] * si).astype(bf16).reshape(4, 16, LANES)
+                    co = tw[f, after[n]]
+                    si = tw[16 + f, after[n]]
+                    cc[n, 2 * f] = (b_re[b] * co - b_im[b] * si).astype(bf16)
+                    cc[n, 2 * f + 1] = (b_im[b] * co + b_re[b] * si).astype(bf16)
 
     def unmix(n):
         def body(v, carry):
-            halves = [cc[n, :, 2 * v + u].reshape(512, LANES) for u in range(2)]
+            rows = [pl.ds(pl.multiple_of(32 * v + 16 * u, 16), 16) for u in range(2)]
+            halves = [cc[n, :, rows[u], :].reshape(512, LANES) for u in range(2)]
             data = jnp.concatenate(halves, axis=1)
             got = (dot(mixbt[0], data) + dot(mixbt[1], data)).reshape(8, 8, 16, 2 * LANES)
             for u in range(2):
-                part[n, :, :, 2 * v + u] = got[:, :, :, LANES * u : LANES * (u + 1)]
+                part[n, :, :, rows[u], :] = got[:, :, :, LANES * u : LANES * (u + 1)]
             return carry
 
         lax.fori_loop(0, 2, body, 0)
@@ -302,29 +318,24 @@
             for way in range(2):
                 wait_bytes(rbuf.at[n, way, 3, piece], rsr.at[n, way, 3, h])
             total = part[n, z, piece] + (rbuf[n, 0, 3, piece].astype(f32) + rbuf[n, 1, 3, piece].astype(f32))
-            fs[n // 2, pl.ds(16 * h, 16), n % 2] = total.astype(bf16).reshape(16, 16, LANES)
-
-    def give_all(g):
-        pltpu.make_async_copy(fs.at[g, 4 * mine + y], fb.at[g, own], s9r.at[g]).start()
-
-        def give(i, carry):
-            xx, c_, yy = peer(i)
+            fs[n, piece] = total.astype(bf16)
+
+    def give_all(k):
+        if k == 0:
+            pltpu.make_async_copy(fs.at[k, mine], fb.at[own], s9r.at[k]).start()
+        for place, seq in plane[k == 0 :]:
             pltpu.make_async_remote_copy(
-                src_ref=fs.at[g, 4 * (2 * xx + c_) + yy], dst_ref=fb.at[g, own],
-                send_sem=s9s.at[g], recv_sem=s9r.at[g],
-                device_id={"seq": seq_of(xx, z, c_), "ch": yy}, device_id_type=MESH,
+                src_ref=fs.at[k, place], dst_ref=fb.at[own], send_sem=s9s, recv_sem=s9r.at[k],
+                device_id={"seq": seq, "ch": after[k]}, device_id_type=MESH,
             ).start()
-            return carry
-
-        lax.fori_loop(1, 32, give, 0)
-
-    def finish(g):
-        wait_bytes(fb.at[g], s9r.at[g])
-        for t in range(16):
-            cols = pl.ds(128 * t, LANES)
-            pair = swap(*(fb[g, 2 * t + i].reshape(32, LANES).astype(f32) for i in range(2)))
+
+    def finish(k):
+        wait_bytes(fb.at[pl.ds(8 * before[k], 8)], s9r.at[k])
+        for t in range(4):
+            cols = columns_of(before[k], t)
+            pair = swap(*(fb[8 * before[k] + 2 * t + i].astype(f32) for i in range(2)))
             for jh in range(2):
-                rows = pl.ds(64 * jh + 32 * g, 32)
+                rows = pl.ds(64 * jh, 64)
                 field = pair[jh] + bias_ref[:, cols] * product_of(rows, cols)
                 out_ref[rows, cols] = (gate_v[rows, cols].astype(f32) * field).astype(bf16)
 
@@ -336,127 +347,136 @@
     for load in loads[2:]:
         load.start()
     s1_wait(0)
-    ag_begin(1, 1)
-    ag_begin(1, 0)
     ag_begin(0, 0)
+    ag_begin(0, 1)
     multiply(1)
     spread_all(1)
-    ag_step(1, 1, 1)
-    ag_begin(0, 1)
     loads[5].wait()
     lax.fori_loop(0, 8, repack, 0)
-    ag_step(1, 1, 0)
-    lax.fori_loop(16, 24, repack, 0)
+    loads[4].wait()
+    lax.fori_loop(0, 4, widen, 0)
     lax.fori_loop(8, 16, repack, 0)
     ag_step(0, 1, 0)
+    multiply(2)
+    spread_all(2)
+    ag_step(0, 1, 1)
+    lax.fori_loop(16, 24, repack, 0)
+    s1_wait(1)
+    ag_begin(1, 0)
+    ag_begin(1, 1)
+    lax.fori_loop(4, 8, widen, 0)
+    ag_step(0, 2, 0)
+    multiply(3)
+    spread_all(3)
     lax.fori_loop(24, 32, repack, 0)
+    ag_step(0, 2, 1)
     filter_send()
-    ag_step(1, 2, 1)
+    lax.fori_loop(8, 12, widen, 0)
+    ag_step(1, 1, 0)
     loads[2].wait()
     spread_table(mix_s, mixb)
-    ag_step(0, 1, 1)
-    loads[4].wait()
-    lax.fori_loop(0, 4, widen, 0)
+    ag_step(1, 1, 1)
+    lax.fori_loop(12, 16, widen, 0)
+    ag_step(0, 3, 0)
     loads[3].wait()
     spread_table(mixt_s, mixbt)
+    ag_step(0, 3, 1)
+    s1_wait(2)
+    ag_begin(2, 0)
     ag_step(1, 2, 0)
-    ag_step(0, 2, 0)
-    lax.fori_loop(4, 8, widen, 0)
-    lax.fori_loop(12, 16, widen, 0)
+    ag_step(1, 2, 1)
+    ag_end(0)
+    mix(0)
+    ag_step(2, 1, 0)
+    ag_begin(2, 1)
+    ag_step(1, 3, 0)
+    s1_wait(3)
+    ag_begin(3, 0)
     ag_step(1, 3, 1)
-    lax.fori_loop(8, 12, widen, 0)
-    s1_wait(1)
+    ag_step(2, 2, 0)
+    ag_step(2, 1, 1)
     ag_begin(3, 1)
-    ag_step(0, 2, 1)
-    ag_step(1, 3, 0)
-    ag_step(0, 3, 0)
-    ag_begin(3, 0)
-    ag_step(3, 1, 1)
-    ag_step(0, 3, 1)
+    ag_step(3, 1, 0)
     ag_end(1)
     mix(1)
-    ag_begin(2, 1)
-    ag_begin(2, 0)
-    ag_step(3, 1, 0)
+    ag_step(2, 3, 0)
+    loads[6].wait()
+    forward(0, 2)
+    forward(0, 0)
+    forward(0, 1)
+    ag_step(2, 2, 1)
+    forward(0, 3)
+    ag_step(3, 1, 1)
+    ag_step(3, 2, 0)
+    ag_step(2, 3, 1)
     ag_step(3, 2, 1)
-    ag_end(0)
-    mix(0)
-    ag_step(2, 1, 1)
-    loads[6].wait()
-    forward(0, 1)
-    forward(0, 0)
-    ag_step(2, 1, 0)
-    forward(0, 2)
-    forward(0, 3)
-    ag_step(3, 2, 0)
+    ag_step(3, 3, 0)
+    ag_end(2)
+    mix(2)
     ag_step(3, 3, 1)
-    ag_step(2, 2, 1)
-    ag_step(2, 2, 0)
-    ag_step(3, 3, 0)
-    ag_step(2, 3, 1)
-    ag_step(2, 3, 0)
     ag_end(3)
     mix(3)
-    ag_end(2)
-    mix(2)
     wait_bytes(hh, hsr)
+    forward(1, 1)
+    forward(1, 3)
     forward(1, 0)
     forward(1, 2)
-    forward(1, 1)
-    forward(1, 3)
     inverse(0)
     unmix(0)
+    rs_step(0, 1, 0)
     rs_step(0, 1, 1)
-    rs_step(0, 1, 0)
     inverse(1)
     inverse(2)
+    rs_step(0, 2, 0)
+    unmix(1)
     rs_step(0, 2, 1)
-    rs_step(0, 2, 0)
-    unmix(2)
-    rs_step(2, 1, 1)
-    rs_step(2, 1, 0)
-    rs_step(0, 3, 1)
-    unmix(1)
-    rs_step(0, 3, 0)
-    rs_step(2, 2, 1)
-    inverse(3)
-    rs_step(2, 2, 0)
-    unmix(3)
-    rs_step(0, 4, 1)
-    rs_step(0, 4, 0)
-    rs_step(2, 3, 1)
-    rs_step(2, 3, 0)
     rs_step(1, 1, 0)
     rs_step(1, 1, 1)
-    rs_end(0)
-    rs_step(3, 1, 1)
-    rs_step(3, 1, 0)
-    rs_step(2, 4, 1)
-    rs_step(2, 4, 0)
+    rs_step(0, 3, 0)
+    unmix(2)
+    rs_step(0, 3, 1)
+    inverse(3)
     rs_step(1, 2, 0)
     rs_step(1, 2, 1)
-    rs_step(3, 2, 1)
-    rs_step(3, 2, 0)
-    rs_end(2)
+    unmix(3)
+    rs_step(0, 4, 0)
+    rs_step(0, 4, 1)
     rs_step(1, 3, 0)
     rs_step(1, 3, 1)
-    rs_step(3, 3, 1)
-    rs_step(3, 3, 0)
+    rs_step(2, 1, 0)
+    rs_step(2, 1, 1)
+    rs_end(0)
+    give_all(0)
+    rs_step(3, 1, 0)
     rs_step(1, 4, 0)
+    rs_step(3, 1, 1)
     rs_step(1, 4, 1)
-    rs_step(3, 4, 1)
-    rs_step(3, 4, 0)
-    rs_end(1)
-    give_all(0)
-    rs_end(3)
-    give_all(1)
+    rs_step(2, 2, 0)
+    rs_step(2, 2, 1)
     loads[7].wait()
     finish(0)
+    rs_step(3, 2, 0)
+    rs_step(3, 2, 1)
+    rs_end(1)
+    give_all(1)
+    rs_step(2, 3, 0)
+    rs_step(2, 3, 1)
+    rs_step(3, 3, 0)
     finish(1)
-
-    for g in range(2):
-        wait_bytes(prod.at[g, pl.ds(0, 31)], s1s.at[g])
-        wait_bytes(prod.at[g, pl.ds(0, 31)], s9s.at[g])
+    rs_step(3, 3, 1)
+    rs_step(2, 4, 0)
+    rs_step(2, 4, 1)
+    rs_step(3, 4, 0)
+    rs_step(3, 4, 1)
+    rs_end(2)
+    give_all(2)
+    rs_end(3)
+    give_all(3)
+    finish(2)
+    finish(3)
+
+    wait_bytes(prod.at[pl.ds(0, 31)], s1s)
+    wait_bytes(prod.at[pl.ds(0, 31)], s9s)
     wait_bytes(hs.at[pl.ds(0, 7)], hss)
     for n in range(4):
         wait_bytes(gath.at[n, pl.ds(0, 7)], ags.at[n])
@@ -483,28 +503,28 @@
             pltpu.VMEM((2, 32, 64), bf16),
             pltpu.VMEM((2, 64, 32), bf16),
             pltpu.VMEM((2, 32, 128), f32),
-            pltpu.VMEM((2, 32, 2, 16, LANES), bf16),
-            pltpu.VMEM((4, NZ, 8, 4, 16, LANES), bf16),
+            pltpu.VMEM((32, 64, LANES), bf16),
+            pltpu.VMEM((4, NZ, 8, 64, LANES), bf16),
             pltpu.VMEM((2, 512, 1024), bf16),
             pltpu.VMEM((2, 1024, 512), bf16),
             pltpu.VMEM((32, 4, 64, LANES), f32),
-            pltpu.VMEM((2, 8, 2, 2, 2, 4, 16, LANES), bf16),
+            pltpu.VMEM((2, 8, 4, 2, 64, LANES), bf16),
             pltpu.VMEM((2, 4, 512, 2 * LANES), f32),
             pltpu.VMEM((2, 4, 512, 2 * LANES), bf16),
-            pltpu.VMEM((4, 32, 4, 16, LANES), bf16),
-            pltpu.VMEM((4, NZ, 8, 4, 16, LANES), f32),
-            pltpu.VMEM((4, 2, 4, 8, 4, 16, LANES), bf16),
-            pltpu.VMEM((4, 2, 4, 8, 4, 16, LANES), bf16),
+            pltpu.VMEM((4, 32, 64, LANES), bf16),
+            pltpu.VMEM((4, NZ, 8, 64, LANES), f32),
+            pltpu.VMEM((4, 2, 4, 8, 64, LANES), bf16),
+            pltpu.VMEM((4, 2, 4, 8, 64, LANES), bf16),
             pltpu.VMEM((8, 2, 512, LANES), bf16),
             pltpu.VMEM((8, 2, 512, LANES), bf16),
-            pltpu.VMEM((2, 32, 2, 16, LANES), bf16),
-            pltpu.VMEM((2, 32, 2, 16, LANES), bf16),
+            pltpu.VMEM((4, 8, 64, LANES), bf16),
+            pltpu.VMEM((32, 64, LANES), bf16),
             dma((8,)),
-            dma((2,)), dma((2,)),
+            dma, dma((4,)),
             dma((4,)), dma((4, 2, 4, 2)),
             dma, dma,
             dma((4,)), dma((4, 2, 4, 2)),
-            dma((2,)), dma((2,)),
+            dma, dma((4,)),
         ],
         compiler_params=pltpu.CompilerParams(
             collective_id=0, has_side_effects=True, vmem_limit_bytes=60 * 1024 * 1024

time: 119 us -> 119 us (level)
  no operation moved by 1% of the time
where the time goes in v5:
time: 119 us
  Pallas kernels  117 us (98%)
  local copies, waits for them, and re-layouts  1.88 us (2%)
    pallas_call x1, Pallas kernels, per_device(): pl.pallas_call(kernel, out_shape=jax.ShapeDtypeStruct((rows, width), bf16...  117 us

profile of v5, /device:TPU:1, one launch (start us, length us, event | category | flops | bytes accessed | tf_op | source)
XLA Modules:
  0.0 119.3 jit_solution(4648830079984830932)
XLA Ops:
  0.0 117.4 %hyena.1 = bf16[128,2048]{1,0:T(8,128)(2,1)} custom-call(bf16[128,2048]{1,0:T(8,128)(2,1)} %gate_in.1, bf16[128,2048]{1,0:T(8,128)(2,1)} %key_in.1, bf16[128,2048]{1,0:T(8,128)(2,1)} %value_in.1, f32[2,2,512,512]{3,2,1,0:T(8,128)} %spec_in.1, bf16[1,2,512,512]{3,2,1,0:T(8,128)(2,1)} %constant.8.clone.cs_in, bf16[8,2,32,64]{3,2,1,0:T(8,128)(2,1)} %constant.9.clone.mix_in, ...), custom_call_target="tpu_custom_call" | custom-call | tf_op jit(solution)/shard_map/hyena/pallas_call | solution.py:492
  117.4 1.9 %copy.11 = bf16[128,2048]{1,0:T(8,128)(2,1)} copy(bf16[128,2048]{1,0:T(8,128)(2,1)} %hyena.1) | data formatting | bytes 1048576

commit v6 on v5

--- a/solution.py
+++ b/solution.py
@@ -344,129 +344,129 @@
     multiply(0)
     pl.semaphore_wait(barrier, 33)
     spread_all(0)
+    multiply(1)
+    spread_all(1)
+    multiply(2)
+    spread_all(2)
+    multiply(3)
+    spread_all(3)
     for load in loads[2:]:
         load.start()
     s1_wait(0)
     ag_begin(0, 0)
     ag_begin(0, 1)
-    multiply(1)
-    spread_all(1)
     loads[5].wait()
     lax.fori_loop(0, 8, repack, 0)
     loads[4].wait()
     lax.fori_loop(0, 4, widen, 0)
     lax.fori_loop(8, 16, repack, 0)
     ag_step(0, 1, 0)
-    multiply(2)
-    spread_all(2)
-    ag_step(0, 1, 1)
-    lax.fori_loop(16, 24, repack, 0)
+    lax.fori_loop(4, 8, widen, 0)
     s1_wait(1)
     ag_begin(1, 0)
     ag_begin(1, 1)
-    lax.fori_loop(4, 8, widen, 0)
+    ag_step(0, 1, 1)
+    lax.fori_loop(16, 24, repack, 0)
+    s1_wait(2)
+    ag_begin(2, 0)
+    ag_begin(2, 1)
+    lax.fori_loop(8, 12, widen, 0)
     ag_step(0, 2, 0)
-    multiply(3)
-    spread_all(3)
+    loads[3].wait()
+    spread_table(mixt_s, mixbt)
+    ag_step(1, 1, 0)
     lax.fori_loop(24, 32, repack, 0)
+    ag_step(1, 1, 1)
+    s1_wait(3)
+    ag_begin(3, 0)
+    ag_begin(3, 1)
+    filter_send()
     ag_step(0, 2, 1)
-    filter_send()
-    lax.fori_loop(8, 12, widen, 0)
-    ag_step(1, 1, 0)
+    lax.fori_loop(12, 16, widen, 0)
+    ag_step(2, 1, 0)
     loads[2].wait()
     spread_table(mix_s, mixb)
-    ag_step(1, 1, 1)
-    lax.fori_loop(12, 16, widen, 0)
+    ag_step(2, 1, 1)
     ag_step(0, 3, 0)
-    loads[3].wait()
-    spread_table(mixt_s, mixbt)
-    ag_step(0, 3, 1)
-    s1_wait(2)
-    ag_begin(2, 0)
     ag_step(1, 2, 0)
     ag_step(1, 2, 1)
+    ag_step(3, 1, 0)
+    ag_step(3, 1, 1)
+    ag_step(0, 3, 1)
+    ag_step(2, 2, 0)
+    ag_step(2, 2, 1)
+    ag_step(1, 3, 0)
+    ag_step(1, 3, 1)
+    ag_step(3, 2, 0)
+    ag_step(3, 2, 1)
     ag_end(0)
     mix(0)
-    ag_step(2, 1, 0)
-    ag_begin(2, 1)
-    ag_step(1, 3, 0)
-    s1_wait(3)
-    ag_begin(3, 0)
-    ag_step(1, 3, 1)
-    ag_step(2, 2, 0)
-    ag_step(2, 1, 1)
-    ag_begin(3, 1)
-    ag_step(3, 1, 0)
+    ag_step(2, 3, 0)
+    ag_step(2, 3, 1)
     ag_end(1)
     mix(1)
-    ag_step(2, 3, 0)
+    ag_step(3, 3, 0)
     loads[6].wait()
+    forward(0, 3)
+    forward(0, 0)
+    ag_step(3, 3, 1)
     forward(0, 2)
-    forward(0, 0)
     forward(0, 1)
-    ag_step(2, 2, 1)
-    forward(0, 3)
-    ag_step(3, 1, 1)
-    ag_step(3, 2, 0)
-    ag_step(2, 3, 1)
-    ag_step(3, 2, 1)
-    ag_step(3, 3, 0)
     ag_end(2)
     mix(2)
-    ag_step(3, 3, 1)
     ag_end(3)
     mix(3)
     wait_bytes(hh, hsr)
+    forward(1, 0)
+    forward(1, 3)
     forward(1, 1)
-    forward(1, 3)
-    forward(1, 0)
     forward(1, 2)
     inverse(0)
     unmix(0)
     rs_step(0, 1, 0)
     rs_step(0, 1, 1)
     inverse(1)
+    unmix(1)
+    rs_step(1, 1, 0)
+    rs_step(0, 2, 0)
+    rs_step(1, 1, 1)
+    rs_step(0, 2, 1)
     inverse(2)
-    rs_step(0, 2, 0)
-    unmix(1)
-    rs_step(0, 2, 1)
-    rs_step(1, 1, 0)
-    rs_step(1, 1, 1)
+    unmix(2)
+    rs_step(1, 2, 0)
     rs_step(0, 3, 0)
-    unmix(2)
+    rs_step(2, 1, 0)
+    rs_step(1, 2, 1)
+    rs_step(2, 1, 1)
+    inverse(3)
     rs_step(0, 3, 1)
-    inverse(3)
-    rs_step(1, 2, 0)
-    rs_step(1, 2, 1)
     unmix(3)
+    rs_step(1, 3, 0)
     rs_step(0, 4, 0)
+    rs_step(2, 2, 0)
+    rs_step(3, 1, 0)
+    rs_step(3, 1, 1)
+    rs_step(1, 3, 1)
+    rs_step(2, 2, 1)
     rs_step(0, 4, 1)
-    rs_step(1, 3, 0)
-    rs_step(1, 3, 1)
-    rs_step(2, 1, 0)
-    rs_step(2, 1, 1)
+    rs_step(1, 4, 0)
+    rs_step(2, 3, 0)
+    rs_step(3, 2, 0)
+    rs_step(3, 2, 1)
+    rs_step(1, 4, 1)
+    rs_step(2, 3, 1)
     rs_end(0)
     give_all(0)
-    rs_step(3, 1, 0)
-    rs_step(1, 4, 0)
-    rs_step(3, 1, 1)
-    rs_step(1, 4, 1)
-    rs_step(2, 2, 0)
-    rs_step(2, 2, 1)
+    rs_step(2, 4, 0)
+    rs_step(3, 3, 0)
     loads[7].wait()
     finish(0)
-    rs_step(3, 2, 0)
-    rs_step(3, 2, 1)
+    rs_step(3, 3, 1)
     rs_end(1)
     give_all(1)
-    rs_step(2, 3, 0)
-    rs_step(2, 3, 1)
-    rs_step(3, 3, 0)
-    finish(1)
-    rs_step(3, 3, 1)
-    rs_step(2, 4, 0)
     rs_step(2, 4, 1)
     rs_step(3, 4, 0)
+    finish(1)
     rs_step(3, 4, 1)
     rs_end(2)
     give_all(2)

time: 119 us -> 119 us (level)
  no operation moved by 1% of the time
where the time goes in v6:
time: 119 us
  Pallas kernels  117 us (98%)
  local copies, waits for them, and re-layouts  1.88 us (2%)
    pallas_call x1, Pallas kernels, per_device(): pl.pallas_call(kernel, out_shape=jax.ShapeDtypeStruct((rows, width), bf16...  117 us

profile of v6, /device:TPU:1, one launch (start us, length us, event | category | flops | bytes accessed | tf_op | source)
XLA Modules:
  0.0 118.7 jit_solution(4916396191800958278)
XLA Ops:
  0.0 116.8 %hyena.1 = bf16[128,2048]{1,0:T(8,128)(2,1)} custom-call(bf16[128,2048]{1,0:T(8,128)(2,1)} %gate_in.1, bf16[128,2048]{1,0:T(8,128)(2,1)} %key_in.1, bf16[128,2048]{1,0:T(8,128)(2,1)} %value_in.1, f32[2,2,512,512]{3,2,1,0:T(8,128)} %spec_in.1, bf16[1,2,512,512]{3,2,1,0:T(8,128)(2,1)} %constant.8.clone.cs_in, bf16[8,2,32,64]{3,2,1,0:T(8,128)(2,1)} %constant.9.clone.mix_in, ...), custom_call_target="tpu_custom_call" | custom-call | tf_op jit(solution)/shard_map/hyena/pallas_call | solution.py:492
  116.8 1.9 %copy.11 = bf16[128,2048]{1,0:T(8,128)(2,1)} copy(bf16[128,2048]{1,0:T(8,128)(2,1)} %hyena.1) | data formatting | bytes 1048576

commit v7 on v6

--- a/solution.py
+++ b/solution.py
@@ -290,6 +290,20 @@
             got = (dot(mixbt[0], data) + dot(mixbt[1], data)).reshape(8, 8, 16, 2 * LANES)
             for u in range(2):
                 part[n, :, :, rows[u], :] = got[:, :, :, LANES * u : LANES * (u + 1)]
+            return carry
+
+        lax.fori_loop(0, 2, body, 0)
+
+    def unmix_first(n):
+        far = lax.rem(z + NZ // 2, NZ)
+        at = pl.ds(pl.multiple_of(128 * far, 128), 128)
+
+        def body(v, carry):
+            rows = [pl.ds(pl.multiple_of(32 * v + 16 * u, 16), 16) for u in range(2)]
+            data = jnp.concatenate([cc[n, :, rows[u], :].reshape(512, LANES) for u in range(2)], axis=1)
+            got = (dot(mixbt[0, at, :], data) + dot(mixbt[1, at, :], data)).reshape(8, 16, 2 * LANES)
+            for u in range(2):
+                part[n, far, :, rows[u], :] = got[:, :, LANES * u : LANES * (u + 1)]
             return carry
 
         lax.fori_loop(0, 2, body, 0)
@@ -422,9 +436,10 @@
     forward(1, 1)
     forward(1, 2)
     inverse(0)
-    unmix(0)
+    unmix_first(0)
     rs_step(0, 1, 0)
     rs_step(0, 1, 1)
+    unmix(0)
     inverse(1)
     unmix(1)
     rs_step(1, 1, 0)

time: 119 us -> 118 us (level)
  Pallas kernels: 117 us -> 115 us
    pallas_call x1, Pallas kernels: 117 us -> 115 us  [per_device(): pl.pallas_call(kernel, out_shape=jax.ShapeDtypeStruct((rows, width), bf16...]
where the time goes in v7:
time: 118 us; the launch traced here: 117 us
  Pallas kernels  115 us (97%)
  local copies, waits for them, and re-layouts  1.88 us (2%)
    pallas_call x1, Pallas kernels, per_device(): pl.pallas_call(kernel, out_shape=jax.ShapeDtypeStruct((rows, width), bf16...  115 us

profile of v7, /device:TPU:1, one launch (start us, length us, event | category | flops | bytes accessed | tf_op | source)
XLA Modules:
  0.0 117.3 jit_solution(16898643003168335059)
XLA Ops:
  0.0 115.4 %hyena.1 = bf16[128,2048]{1,0:T(8,128)(2,1)} custom-call(bf16[128,2048]{1,0:T(8,128)(2,1)} %gate_in.1, bf16[128,2048]{1,0:T(8,128)(2,1)} %key_in.1, bf16[128,2048]{1,0:T(8,128)(2,1)} %value_in.1, f32[2,2,512,512]{3,2,1,0:T(8,128)} %spec_in.1, bf16[1,2,512,512]{3,2,1,0:T(8,128)(2,1)} %constant.8.clone.cs_in, bf16[8,2,32,64]{3,2,1,0:T(8,128)(2,1)} %constant.9.clone.mix_in, ...), custom_call_target="tpu_custom_call" | custom-call | tf_op jit(solution)/shard_map/hyena/pallas_call | solution.py:507
  115.4 1.9 %copy.11 = bf16[128,2048]{1,0:T(8,128)(2,1)} copy(bf16[128,2048]{1,0:T(8,128)(2,1)} %hyena.1) | data formatting | bytes 1048576
